TPU v7x, 128 devices: a whole 4x4x4 slice. The times are simulated.
128 devices in a mesh: section: 2 (over core), lat: 32 (over x, y, z_lo), dp: 2 (over z_hi).
Axes of the slice: x: 4, y: 4, z: 4 (z_hi: 2, z_lo: 2; z = z_hi * 2 + z_lo), core: 2. Of those that a mesh axis runs over, the one named last changes fastest.
Arguments:
- volume: bfloat16 [8, 32, 64, 8, 256], P('dp', None, 'lat'), may hold values from -6 to 6
- cotangent: bfloat16 [8, 32, 64, 8, 256], P('dp', None, 'lat'), may hold values from -6 to 6
- weights: bfloat16 [2, 32, 32, 3, 3, 3], P('section'), may hold values from -0.21875 to 0.21875
Outputs:
- level_field: bfloat16 [2, 8, 32, 64, 8, 256], P('section', 'dp', None, 'lat')
- weight_grads: float32 [2, 32, 32, 3, 3, 3], P('section')
All inputs are finite; a program needn't handle non-finite values.
Results may differ from a plain program's by a relative error of at most 0.0075.
Values may be sent and summed in bfloat16 or wider, within the bound.
No kernel may reach another device: no remote copies, remote signals or barrier semaphores. Data moves between devices by JAX's collectives and lax.ppermute only.
A program may use at most 128 MiB of HBM per device.

v0:
```python
import jax
import jax.numpy as jnp
from jax import lax
from jax.sharding import PartitionSpec as P


def padded_2(block, sides, width):
    for axis, dim in sides:
        count = lax.axis_size(axis)
        forward = [(i, i + 1) for i in range(count - 1)]
        backward = [(target, source) for source, target in forward]
        low = lax.ppermute(
            lax.slice_in_dim(block, block.shape[dim] - width, None, axis=dim), axis, forward
        )
        high = lax.ppermute(lax.slice_in_dim(block, 0, width, axis=dim), axis, backward)
        block = jnp.concatenate([low, block, high], axis=dim)
    return block


def shifted(value, axis, steps):
    count = lax.axis_size(axis)
    initial, last = (max(0, -steps), min(count, count - steps))
    return lax.ppermute(value, axis, [(source, source + steps) for source in range(initial, last)])


def apply_conv(padded, kernel):
    return lax.conv_general_dilated(
        padded,
        kernel,
        (1, 1, 1),
        ((0, 0), (1, 1), (1, 1)),
        dimension_numbers=("NCDHW", "OIDHW", "NCDHW"),
        preferred_element_type=jnp.float32,
    )


def flipped(kernel):
    return jnp.transpose(jnp.flip(kernel, (2, 3, 4)), (1, 0, 2, 3, 4))


def kernel_grad(padded, delta):
    raw_grad = lax.conv_general_dilated(
        padded,
        delta,
        (1, 1, 1),
        ((0, 0), (1, 1), (1, 1)),
        dimension_numbers=("CNDHW", "IODHW", "NCDHW"),
        preferred_element_type=jnp.float32,
    )
    return jnp.transpose(raw_grad, (1, 0, 2, 3, 4))


def slope(pre_act):
    sigmoid_val = jax.nn.sigmoid(pre_act)
    return sigmoid_val * (1.0 + pre_act * (1.0 - sigmoid_val))


def level_forward(field, kernel):
    padded = padded_2(field, (("lat", 2),), 1)
    pre_act = apply_conv(padded, kernel)
    result = (field.astype(jnp.float32) + jax.nn.silu(pre_act)).astype(jnp.bfloat16)
    return (result, padded, pre_act)


def level_backward(grad_out, padded, pre_act, kernel):
    delta = (grad_out.astype(jnp.float32) * slope(pre_act)).astype(jnp.bfloat16)
    delta_pad = padded_2(delta, (("lat", 2),), 1)
    back_field = (grad_out.astype(jnp.float32) + apply_conv(delta_pad, flipped(kernel))).astype(
        jnp.bfloat16
    )
    return (back_field, kernel_grad(padded, delta))


def body(volume, cotangent, weights):
    micro_count = volume.shape[0]
    section = lax.axis_index("section")
    first = section == 0
    blank = jnp.zeros_like(volume[0:1])
    kernel = weights[0]
    incoming = blank
    forward_outs = []
    saved = []
    for moment in range(micro_count + 1):
        own_slice = volume[moment : moment + 1] if moment < micro_count else blank
        field = jnp.where(first, own_slice, incoming)
        result, padded, pre_act = level_forward(field, kernel)
        forward_outs.append(result)
        saved.append((padded, pre_act))
        if moment < micro_count:
            incoming = shifted(result, "section", 1)
    returning = blank
    grad_total = jnp.zeros(weights.shape[1:], jnp.float32)
    back_outs = []
    for moment in range(micro_count + 1):
        outer_grad = (
            cotangent[micro_count - 1 - moment : micro_count - moment]
            if moment < micro_count
            else blank
        )
        grad_out = jnp.where(first, returning, outer_grad)
        padded, pre_act = saved[micro_count - moment]
        back_field, grad_term = level_backward(grad_out, padded, pre_act, kernel)
        grad_total = grad_total + grad_term
        back_outs.append(back_field)
        if moment < micro_count:
            returning = shifted(back_field, "section", -1)
    slot_fields = [
        jnp.where(first, back_outs[micro_count - member], forward_outs[member + 1])
        for member in range(micro_count)
    ]
    field_out = jnp.concatenate(slot_fields, 0)[None]
    local_grads = grad_total[None]
    summed = lax.psum(local_grads, ("lat", "dp"))
    return (field_out, summed)


def solution(mesh):
    return jax.shard_map(
        body,
        mesh=mesh,
        in_specs=(
            P("dp", None, "lat", None, None),
            P("dp", None, "lat", None, None),
            P("section", None, None, None, None, None),
        ),
        out_specs=(
            P("section", "dp", None, "lat", None, None),
            P("section", None, None, None, None, None),
        ),
        check_vma=False,
    )
```

profile of v0, /device:TPU:0, one launch (start us, length us, event | category | flops | bytes accessed | tf_op | source)
XLA Modules:
  0.0 713.6 jit_solution(5312781947773473900)
XLA Ops:
  9.6 4.6 collective-permute-start
  15.7 3.0 collective-permute-done
  21.7 4.1 copy.309
  26.7 6.0 fusion.12
  45.4 5.2 collective-permute-start.3
  52.5 3.0 collective-permute-done.3
  58.5 4.1 copy.314
  63.5 6.0 fusion.16
  81.3 5.2 collective-permute-start.6
  88.4 3.0 collective-permute-done.6
  94.4 4.1 copy.319
  99.4 6.0 fusion.20
  117.1 5.3 collective-permute-start.9
  124.2 3.0 collective-permute-done.9
  130.2 4.1 copy.324
  135.3 6.0 fusion.24
  152.1 5.5 collective-permute-start.12
  159.2 3.0 collective-permute-done.12
  165.2 4.1 copy.329
  170.2 6.0 fusion.28
  185.8 5.2 collective-permute-start.14
  192.6 3.0 collective-permute-done.14
  196.9 3.1 reshape.31
  200.0 4.1 copy.334
  205.0 6.0 fusion.32
  213.5 2.5 copy.384
  216.0 2.9 reshape.134
  222.1 2.6 copy.385
  229.4 5.2 collective-permute-start.17
  234.7 2.5 copy.393
  237.2 2.8 reshape.143
  242.2 4.1 copy.341
  247.2 6.0 fusion.36
  255.7 2.5 copy.386
  258.2 2.9 reshape.136
  264.6 2.5 copy.387
  267.2 2.9 reshape.137
  273.8 6.1 collective-permute-start.20
  279.9 2.5 copy.391
  282.4 2.8 reshape.141
  285.2 4.7 copy.376
  289.9 2.5 copy.389
  292.5 2.8 reshape.139
  295.3 4.7 copy.374
  300.1 4.7 copy.372
  304.8 4.7 copy.370
  309.5 2.5 copy.369
  312.0 4.8 copy.368
  316.7 2.5 copy.371
  322.4 4.1 copy.348
  327.4 6.0 fusion.40
  341.3 30.2 %fusion.179 = f32[32,32,3,3,3]{0,1,4,3,2:T(8,128)} fusion(bf16[1,32,4,8,256]{1,0,4,3,2:T(2,128)(2,1)} %copy.370, bf16[1,32,2,8,256]{1,0,4,3,2:T(2,128)(2,1)} %copy.371), kind=kOutput, calls=%fused_computation.231 | convolution fusion | flops 207077376 | bytes 897024 | tf_op jit(solution)/shard_map/transpose | solution.py:50
  376.5 5.5 collective-permute-start.23
  382.0 31.6 %fusion.180 = f32[32,32,3,3,3]{0,1,4,3,2:T(8,128)} fusion(bf16[1,32,4,8,256]{1,0,4,3,2:T(2,128)(2,1)} %copy.372, bf16[1,32,2,8,256]{1,0,4,3,2:T(2,128)(2,1)S(1)} %copy.373), kind=kOutput, calls=%fused_computation.232 | convolution fusion | flops 207077376 | bytes 897024 | tf_op jit(solution)/shard_map/transpose | solution.py:50
  413.6 2.5 copy.375
  419.2 4.1 copy.355
  424.2 5.9 fusion.44
  438.1 30.2 %fusion.181 = f32[32,32,3,3,3]{0,1,4,3,2:T(8,128)} fusion(bf16[1,32,4,8,256]{1,0,4,3,2:T(2,128)(2,1)} %copy.374, bf16[1,32,2,8,256]{1,0,4,3,2:T(2,128)(2,1)} %copy.375), kind=kOutput, calls=%fused_computation.233 | convolution fusion | flops 207077376 | bytes 897024 | tf_op jit(solution)/shard_map/transpose | solution.py:50
  472.6 5.5 collective-permute-start.26
  478.1 31.1 %fusion.182 = f32[32,32,3,3,3]{0,1,4,3,2:T(8,128)S(1)} fusion(bf16[1,32,4,8,256]{1,0,4,3,2:T(2,128)(2,1)} %copy.376, bf16[1,32,2,8,256]{1,0,4,3,2:T(2,128)(2,1)S(1)} %copy.377), kind=kOutput, calls=%fused_computation.234 | convolution fusion | flops 207077376 | bytes 897024 | tf_op jit(solution)/shard_map/transpose | solution.py:50
  509.3 30.6 %fusion.88 = f32[1,32,32,3,3,3]{1,2,5,4,3,0:T(8,128)} fusion(f32[32,32,3,3,3]{0,1,4,3,2:T(8,128)S(1)} %fusion.182, f32[32,32,3,3,3]{0,1,4,3,2:T(8,128)S(1)} %copy-done.37, f32[32,32,3,3,3]{0,1,4,3,2:T(8,128)S(1)} %copy-done.36, f32[32,32,3,3,3]{0,1,4,3,2:T(8,128)S(1)} %copy-done.35, bf16[1,32,4,8,256]{1,0,4,3,2:T(2,128)(2,1)S(1)} %copy-done.6, ...), kind=kOutput, calls=%fused_computation.90 | convolution fusion | flops 207187968 | bytes 1339392 | tf_op jit(solution)/shard_map/transpose | solution.py:50
  539.9 142.5 %all-reduce.2.cloned.1.call-done = f32[1,32,32,3,3,3]{1,2,5,4,3,0:T(8,128)} async-done(((f32[1,32,32,3,3,3]{1,2,5,4,3,0:T(8,128)}), f32[1,32,32,3,3,3]{1,2,5,4,3,0:T(8,128)}) %all-reduce.2.cloned.1.call-update) | async-done | bytes 110608 | tf_op jit(solution)/shard_map/psum | solution.py:113
  687.6 4.1 copy.362
  692.6 6.0 fusion.48
  (227 shorter events, 161.4 us)
Async XLA Ops:
  7.2 19.5 %copy-start = (bf16[1,32,32,3,3,3]{2,1,5,4,3,0:T(8,128)(2,1)S(1)}, bf16[1,32,32,3,3,3]{2,1,5,4,3,0:T(8,128)(2,1)}, u32[]{:S(2)}) copy-start(bf16[1,32,32,3,3,3]{2,1,5,4,3,0:T(8,128)(2,1)} %param.5) | copy-start | bytes 165892
  7.2 675.2 %all-reduce.2.cloned.1.call-start = ((), (), s32[]{:S(2)}) async-start(), calls=%async_computation | async-start | bytes 884736 | tf_op jit(solution)/shard_map/psum | solution.py:113
  8.3 7.4 %collective-permute-start.1 = (bf16[1,32,1,8,256]{4,3,2,1,0:T(8,128)(2,1)S(1)}, bf16[1,32,1,8,256]{4,3,2,1,0:T(8,128)(2,1)S(1)}, u32[]{:S(2)}, u32[]{:S(2)}) collective-permute-start(bf16[1,32,1,8,256]{4,3,2,1,0:T(8,128)(2,1)S(1)} %get-tuple-element.57), channel_id=1, source_target_pairs={{2,0},{4,2},{6,4},{8,6},{10,8},{12,10},{14,12},{16,14},{18,16},{20... | collective-permute-start | bytes 393224 | tf_op jit(solution)/shard_map/ppermute | solution.py:15
  9.6 9.1 %collective-permute-start = (bf16[1,32,1,8,256]{4,3,2,1,0:T(8,128)(2,1)S(1)}, bf16[1,32,1,8,256]{4,3,2,1,0:T(8,128)(2,1)S(1)}, u32[]{:S(2)}, u32[]{:S(2)}) collective-permute-start(bf16[1,32,1,8,256]{4,3,2,1,0:T(8,128)(2,1)S(1)} %get-tuple-element.56), channel_id=1, source_target_pairs={{0,2},{2,4},{4,6},{6,8},{8,10},{10,12},{12,14},{14,16},{16,18},{18... | collective-permute-start | bytes 393224 | tf_op jit(solution)/shard_map/ppermute | solution.py:12
  32.7 2.3 copy-start.32
  40.0 3.1 collective-permute-start.2
  44.1 8.4 %collective-permute-start.4 = (bf16[1,32,1,8,256]{4,3,2,1,0:T(8,128)(2,1)S(1)}, bf16[1,32,1,8,256]{4,3,2,1,0:T(8,128)(2,1)S(1)}, u32[]{:S(2)}, u32[]{:S(2)}) collective-permute-start(bf16[1,32,1,8,256]{4,3,2,1,0:T(8,128)(2,1)S(1)} %get-tuple-element.55), channel_id=1, source_target_pairs={{2,0},{4,2},{6,4},{8,6},{10,8},{12,10},{14,12},{16,14},{18,16},{20... | collective-permute-start | bytes 393224 | tf_op jit(solution)/shard_map/ppermute | solution.py:15
  45.4 10.1 %collective-permute-start.3 = (bf16[1,32,1,8,256]{4,3,2,1,0:T(8,128)(2,1)S(1)}, bf16[1,32,1,8,256]{4,3,2,1,0:T(8,128)(2,1)S(1)}, u32[]{:S(2)}, u32[]{:S(2)}) collective-permute-start(bf16[1,32,1,8,256]{4,3,2,1,0:T(8,128)(2,1)S(1)} %get-tuple-element.54), channel_id=1, source_target_pairs={{0,2},{2,4},{4,6},{6,8},{8,10},{10,12},{12,14},{14,16},{16,18},{18... | collective-permute-start | bytes 393224 | tf_op jit(solution)/shard_map/ppermute | solution.py:12
  75.9 12.5 %copy-start.25 = (bf16[1,32,2,8,256]{4,3,2,1,0:T(8,128)(2,1)}, bf16[1,32,2,8,256]{4,3,2,1,0:T(8,128)(2,1)S(1)}, u32[]{:S(2)}) copy-start(bf16[1,32,2,8,256]{4,3,2,1,0:T(8,128)(2,1)S(1)} %fusion.116) | copy-start | bytes 786436
  75.9 3.1 collective-permute-start.5
  80.0 8.4 %collective-permute-start.7 = (bf16[1,32,1,8,256]{4,3,2,1,0:T(8,128)(2,1)S(1)}, bf16[1,32,1,8,256]{4,3,2,1,0:T(8,128)(2,1)S(1)}, u32[]{:S(2)}, u32[]{:S(2)}) collective-permute-start(bf16[1,32,1,8,256]{4,3,2,1,0:T(8,128)(2,1)S(1)} %get-tuple-element.53), channel_id=1, source_target_pairs={{2,0},{4,2},{6,4},{8,6},{10,8},{12,10},{14,12},{16,14},{18,16},{20... | collective-permute-start | bytes 393224 | tf_op jit(solution)/shard_map/ppermute | solution.py:15
  81.3 10.1 %collective-permute-start.6 = (bf16[1,32,1,8,256]{4,3,2,1,0:T(8,128)(2,1)S(1)}, bf16[1,32,1,8,256]{4,3,2,1,0:T(8,128)(2,1)S(1)}, u32[]{:S(2)}, u32[]{:S(2)}) collective-permute-start(bf16[1,32,1,8,256]{4,3,2,1,0:T(8,128)(2,1)S(1)} %get-tuple-element.52), channel_id=1, source_target_pairs={{0,2},{2,4},{4,6},{6,8},{8,10},{10,12},{12,14},{14,16},{16,18},{18... | collective-permute-start | bytes 393224 | tf_op jit(solution)/shard_map/ppermute | solution.py:12
  111.7 12.5 %copy-start.29 = (bf16[1,32,2,8,256]{4,3,2,1,0:T(8,128)(2,1)}, bf16[1,32,2,8,256]{4,3,2,1,0:T(8,128)(2,1)S(1)}, u32[]{:S(2)}) copy-start(bf16[1,32,2,8,256]{4,3,2,1,0:T(8,128)(2,1)S(1)} %fusion.114) | copy-start | bytes 786436
  111.7 3.1 collective-permute-start.8
  115.8 8.4 %collective-permute-start.10 = (bf16[1,32,1,8,256]{4,3,2,1,0:T(8,128)(2,1)S(1)}, bf16[1,32,1,8,256]{4,3,2,1,0:T(8,128)(2,1)S(1)}, u32[]{:S(2)}, u32[]{:S(2)}) collective-permute-start(bf16[1,32,1,8,256]{4,3,2,1,0:T(8,128)(2,1)S(1)} %get-tuple-element.51), channel_id=1, source_target_pairs={{2,0},{4,2},{6,4},{8,6},{10,8},{12,10},{14,12},{16,14},{18,16},{20... | collective-permute-start | bytes 393224 | tf_op jit(solution)/shard_map/ppermute | solution.py:15
  117.1 10.1 %collective-permute-start.9 = (bf16[1,32,1,8,256]{4,3,2,1,0:T(8,128)(2,1)S(1)}, bf16[1,32,1,8,256]{4,3,2,1,0:T(8,128)(2,1)S(1)}, u32[]{:S(2)}, u32[]{:S(2)}) collective-permute-start(bf16[1,32,1,8,256]{4,3,2,1,0:T(8,128)(2,1)S(1)} %get-tuple-element.50), channel_id=1, source_target_pairs={{0,2},{2,4},{4,6},{6,8},{8,10},{10,12},{12,14},{14,16},{16,18},{18... | collective-permute-start | bytes 393224 | tf_op jit(solution)/shard_map/ppermute | solution.py:12
  147.6 11.6 %copy-start.31 = (bf16[1,32,2,8,256]{4,3,2,1,0:T(8,128)(2,1)}, bf16[1,32,2,8,256]{4,3,2,1,0:T(8,128)(2,1)S(1)}, u32[]{:S(2)}) copy-start(bf16[1,32,2,8,256]{4,3,2,1,0:T(8,128)(2,1)S(1)} %fusion.112) | copy-start | bytes 786436
  147.6 3.1 collective-permute-start.11
  150.7 8.5 %copy-start.24 = (bf16[1,32,2,8,256]{4,3,2,1,0:T(8,128)(2,1)}, bf16[1,32,2,8,256]{4,3,2,1,0:T(8,128)(2,1)S(1)}, u32[]{:S(2)}) copy-start(bf16[1,32,2,8,256]{4,3,2,1,0:T(8,128)(2,1)S(1)} %collective-permute-done.11) | copy-start | bytes 786436
  150.8 8.4 %collective-permute-start.13 = (bf16[1,32,1,8,256]{4,3,2,1,0:T(8,128)(2,1)S(1)}, bf16[1,32,1,8,256]{4,3,2,1,0:T(8,128)(2,1)S(1)}, u32[]{:S(2)}, u32[]{:S(2)}) collective-permute-start(bf16[1,32,1,8,256]{4,3,2,1,0:T(8,128)(2,1)S(1)} %get-tuple-element.49), channel_id=1, source_target_pairs={{2,0},{4,2},{6,4},{8,6},{10,8},{12,10},{14,12},{16,14},{18,16},{20... | collective-permute-start | bytes 393224 | tf_op jit(solution)/shard_map/ppermute | solution.py:15
  152.1 10.1 %collective-permute-start.12 = (bf16[1,32,1,8,256]{4,3,2,1,0:T(8,128)(2,1)S(1)}, bf16[1,32,1,8,256]{4,3,2,1,0:T(8,128)(2,1)S(1)}, u32[]{:S(2)}, u32[]{:S(2)}) collective-permute-start(bf16[1,32,1,8,256]{4,3,2,1,0:T(8,128)(2,1)S(1)} %get-tuple-element.48), channel_id=1, source_target_pairs={{0,2},{2,4},{4,6},{6,8},{8,10},{10,12},{12,14},{14,16},{16,18},{18... | collective-permute-start | bytes 393224 | tf_op jit(solution)/shard_map/ppermute | solution.py:12
  181.8 1.5 copy-start.11
  184.5 11.1 %copy-start.12 = (bf16[1,32,2,8,256]{4,3,2,1,0:T(8,128)(2,1)}, bf16[1,32,2,8,256]{4,3,2,1,0:T(8,128)(2,1)S(1)}, u32[]{:S(2)}) copy-start(bf16[1,32,2,8,256]{4,3,2,1,0:T(8,128)(2,1)S(1)} %fusion.99) | copy-start | bytes 786436
  184.5 8.1 %collective-permute-start.15 = (bf16[1,32,1,8,256]{4,3,2,1,0:T(8,128)(2,1)S(1)}, bf16[1,32,1,8,256]{4,3,2,1,0:T(8,128)(2,1)S(1)}, u32[]{:S(2)}, u32[]{:S(2)}) collective-permute-start(bf16[1,32,1,8,256]{4,3,2,1,0:T(8,128)(2,1)S(1)} %get-tuple-element.47), channel_id=1, source_target_pairs={{2,0},{4,2},{6,4},{8,6},{10,8},{12,10},{14,12},{16,14},{18,16},{20... | collective-permute-start | bytes 393224 | tf_op jit(solution)/shard_map/ppermute | solution.py:15
  185.8 9.7 %collective-permute-start.14 = (bf16[1,32,1,8,256]{4,3,2,1,0:T(8,128)(2,1)S(1)}, bf16[1,32,1,8,256]{4,3,2,1,0:T(8,128)(2,1)S(1)}, u32[]{:S(2)}, u32[]{:S(2)}) collective-permute-start(bf16[1,32,1,8,256]{4,3,2,1,0:T(8,128)(2,1)S(1)} %get-tuple-element.46), channel_id=1, source_target_pairs={{0,2},{2,4},{4,6},{6,8},{8,10},{10,12},{12,14},{14,16},{16,18},{18... | collective-permute-start | bytes 393224 | tf_op jit(solution)/shard_map/ppermute | solution.py:12
  216.0 6.1 copy-start.4
  220.8 6.2 collective-permute-start.16
  224.7 10.0 %copy-start.5 = (f32[2,8,8,33,32]{3,4,2,1,0:T(8,128)S(1)}, f32[2,8,8,33,32]{3,4,2,1,0:T(8,128)}, u32[]{:S(2)}) copy-start(f32[2,8,8,33,32]{3,4,2,1,0:T(8,128)} %get-tuple-element.25) | copy-start | bytes 1622020
  228.1 11.8 %collective-permute-start.18 = (bf16[1,32,1,8,256]{4,3,2,1,0:T(8,128)(2,1)S(1)}, bf16[1,32,1,8,256]{4,3,2,1,0:T(8,128)(2,1)S(1)}, u32[]{:S(2)}, u32[]{:S(2)}) collective-permute-start(bf16[1,32,1,8,256]{4,3,2,1,0:T(8,128)(2,1)S(1)} %get-tuple-element.45), channel_id=1, source_target_pairs={{2,0},{4,2},{6,4},{8,6},{10,8},{12,10},{14,12},{16,14},{18,16},{20... | collective-permute-start | bytes 393224 | tf_op jit(solution)/shard_map/ppermute | solution.py:15
  229.4 10.6 %collective-permute-start.17 = (bf16[1,32,1,8,256]{4,3,2,1,0:T(8,128)(2,1)S(1)}, bf16[1,32,1,8,256]{4,3,2,1,0:T(8,128)(2,1)S(1)}, u32[]{:S(2)}, u32[]{:S(2)}) collective-permute-start(bf16[1,32,1,8,256]{4,3,2,1,0:T(8,128)(2,1)S(1)} %get-tuple-element.44), channel_id=1, source_target_pairs={{0,2},{2,4},{4,6},{6,8},{8,10},{10,12},{12,14},{14,16},{16,18},{18... | collective-permute-start | bytes 393224 | tf_op jit(solution)/shard_map/ppermute | solution.py:12
  258.2 2.9 copy-start.16
  258.2 6.4 copy-start.3
  263.3 6.7 collective-permute-start.19
  267.2 12.7 %copy-start.1 = (f32[2,8,8,33,32]{3,4,2,1,0:T(8,128)S(1)}, f32[2,8,8,33,32]{3,4,2,1,0:T(8,128)}, u32[]{:S(2)}) copy-start(f32[2,8,8,33,32]{3,4,2,1,0:T(8,128)} %get-tuple-element.18) | copy-start | bytes 1622020
  270.1 9.8 %copy-start.27 = (bf16[1,32,2,8,256]{4,3,2,1,0:T(8,128)(2,1)}, bf16[1,32,2,8,256]{4,3,2,1,0:T(8,128)(2,1)S(1)}, u32[]{:S(2)}) copy-start(bf16[1,32,2,8,256]{4,3,2,1,0:T(8,128)(2,1)S(1)} %collective-permute-done.19) | copy-start | bytes 786436
  271.4 47.8 %copy-start.7 = (bf16[1,32,2,8,256]{4,3,2,1,0:T(8,128)(2,1)}, bf16[1,32,2,8,256]{4,3,2,1,0:T(8,128)(2,1)S(1)}, u32[]{:S(2)}) copy-start(bf16[1,32,2,8,256]{4,3,2,1,0:T(8,128)(2,1)S(1)} %fusion.103) | copy-start | bytes 786436
  272.1 47.1 %collective-permute-start.21 = (bf16[1,32,1,8,256]{4,3,2,1,0:T(8,128)(2,1)}, bf16[1,32,1,8,256]{4,3,2,1,0:T(8,128)(2,1)}, u32[]{:S(2)}, u32[]{:S(2)}) collective-permute-start(bf16[1,32,1,8,256]{4,3,2,1,0:T(8,128)(2,1)} %get-tuple-element.43), channel_id=1, source_target_pairs={{2,0},{4,2},{6,4},{8,6},{10,8},{12,10},{14,12},{16,14},{18,16},{20... | collective-permute-start | bytes 393224 | tf_op jit(solution)/shard_map/ppermute | solution.py:15
  273.8 45.4 %collective-permute-start.20 = (bf16[1,32,1,8,256]{4,3,2,1,0:T(8,128)(2,1)S(1)}, bf16[1,32,1,8,256]{4,3,2,1,0:T(8,128)(2,1)}, u32[]{:S(2)}, u32[]{:S(2)}) collective-permute-start(bf16[1,32,1,8,256]{4,3,2,1,0:T(8,128)(2,1)S(1)} %get-tuple-element.42), channel_id=1, source_target_pairs={{0,2},{2,4},{4,6},{6,8},{8,10},{10,12},{12,14},{14,16},{16,18},{18... | collective-permute-start | bytes 393224 | tf_op jit(solution)/shard_map/ppermute | solution.py:12
  282.4 2.8 copy-start.18
  285.2 4.7 copy-start.2
  292.5 2.8 copy-start.19
  295.3 4.7 copy-start.20
  300.1 4.7 copy-start.21
  304.8 4.7 copy-start.13
  309.5 2.5 copy-start.22
  337.2 1.0 copy-start.28
  340.0 32.7 %collective-permute-start.22 = (bf16[1,32,2,8,256]{4,3,2,1,0:T(8,128)(2,1)}, bf16[1,32,2,8,256]{4,3,2,1,0:T(8,128)(2,1)}, u32[]{:S(2)}, u32[]{:S(2)}) collective-permute-start(bf16[1,32,2,8,256]{4,3,2,1,0:T(8,128)(2,1)} %get-tuple-element.15), channel_id=1, source_target_pairs={{64,0},{65,1},{66,2},{67,3},{68,4},{69,5},{70,6},{71,7},{72,8},{73... | collective-permute-start | bytes 786440 | tf_op jit(solution)/shard_map/ppermute | solution.py:23
  341.3 30.2 %copy-start.8 = (bf16[1,32,2,8,256]{4,3,2,1,0:T(8,128)(2,1)S(1)}, bf16[1,32,2,8,256]{4,3,2,1,0:T(8,128)(2,1)}, u32[]{:S(2)}) copy-start(bf16[1,32,2,8,256]{4,3,2,1,0:T(8,128)(2,1)} %copy-done.7) | copy-start | bytes 786436
  371.4 1.2 copy-start.15
  375.2 40.8 %collective-permute-start.24 = (bf16[1,32,1,8,256]{4,3,2,1,0:T(8,128)(2,1)}, bf16[1,32,1,8,256]{4,3,2,1,0:T(8,128)(2,1)}, u32[]{:S(2)}, u32[]{:S(2)}) collective-permute-start(bf16[1,32,1,8,256]{4,3,2,1,0:T(8,128)(2,1)} %get-tuple-element.41), channel_id=1, source_target_pairs={{2,0},{4,2},{6,4},{8,6},{10,8},{12,10},{14,12},{16,14},{18,16},{20... | collective-permute-start | bytes 393224 | tf_op jit(solution)/shard_map/ppermute | solution.py:15
  376.5 39.5 %collective-permute-start.23 = (bf16[1,32,1,8,256]{4,3,2,1,0:T(8,128)(2,1)}, bf16[1,32,1,8,256]{4,3,2,1,0:T(8,128)(2,1)}, u32[]{:S(2)}, u32[]{:S(2)}) collective-permute-start(bf16[1,32,1,8,256]{4,3,2,1,0:T(8,128)(2,1)} %get-tuple-element.40), channel_id=1, source_target_pairs={{0,2},{2,4},{4,6},{6,8},{8,10},{10,12},{12,14},{14,16},{16,18},{18... | collective-permute-start | bytes 393224 | tf_op jit(solution)/shard_map/ppermute | solution.py:12
  382.0 31.6 %copy-start.10 = (bf16[1,32,2,8,256]{4,3,2,1,0:T(8,128)(2,1)S(1)}, bf16[1,32,2,8,256]{4,3,2,1,0:T(8,128)(2,1)}, u32[]{:S(2)}) copy-start(bf16[1,32,2,8,256]{4,3,2,1,0:T(8,128)(2,1)} %copy-done.9) | copy-start | bytes 786436
  430.1 2.3 copy-start.33
  436.8 31.5 %collective-permute-start.25 = (bf16[1,32,2,8,256]{4,3,2,1,0:T(8,128)(2,1)}, bf16[1,32,2,8,256]{4,3,2,1,0:T(8,128)(2,1)}, u32[]{:S(2)}, u32[]{:S(2)}) collective-permute-start(bf16[1,32,2,8,256]{4,3,2,1,0:T(8,128)(2,1)} %get-tuple-element.13), channel_id=1, source_target_pairs={{64,0},{65,1},{66,2},{67,3},{68,4},{69,5},{70,6},{71,7},{72,8},{73... | collective-permute-start | bytes 786440 | tf_op jit(solution)/shard_map/ppermute | solution.py:23
  438.1 30.2 %copy-start.17 = (f32[2,8,1,264,32]{3,1,0,4,2:T(8,128)S(1)}, f32[2,8,1,264,32]{3,1,0,4,2:T(8,128)}, u32[]{:S(2)}) copy-start(f32[2,8,1,264,32]{3,1,0,4,2:T(8,128)} %reshape.141) | copy-start | bytes 1622020
  469.3 39.9 %copy-start.14 = (bf16[1,32,2,8,256]{4,3,2,1,0:T(8,128)(2,1)}, bf16[1,32,2,8,256]{4,3,2,1,0:T(8,128)(2,1)S(1)}, u32[]{:S(2)}) copy-start(bf16[1,32,2,8,256]{4,3,2,1,0:T(8,128)(2,1)S(1)} %fusion.107) | copy-start | bytes 786436
  471.3 213.0 %collective-permute-start.27 = (bf16[1,32,1,8,256]{4,3,2,1,0:T(8,128)(2,1)}, bf16[1,32,1,8,256]{4,3,2,1,0:T(8,128)(2,1)}, u32[]{:S(2)}, u32[]{:S(2)}) collective-permute-start(bf16[1,32,1,8,256]{4,3,2,1,0:T(8,128)(2,1)} %get-tuple-element.39), channel_id=1, source_target_pairs={{2,0},{4,2},{6,4},{8,6},{10,8},{12,10},{14,12},{16,14},{18,16},{20... | collective-permute-start | bytes 393224 | tf_op jit(solution)/shard_map/ppermute | solution.py:15
  472.6 211.7 %collective-permute-start.26 = (bf16[1,32,1,8,256]{4,3,2,1,0:T(8,128)(2,1)}, bf16[1,32,1,8,256]{4,3,2,1,0:T(8,128)(2,1)}, u32[]{:S(2)}, u32[]{:S(2)}) collective-permute-start(bf16[1,32,1,8,256]{4,3,2,1,0:T(8,128)(2,1)} %get-tuple-element.38), channel_id=1, source_target_pairs={{0,2},{2,4},{4,6},{6,8},{8,10},{10,12},{12,14},{14,16},{16,18},{18... | collective-permute-start | bytes 393224 | tf_op jit(solution)/shard_map/ppermute | solution.py:12
  478.1 31.1 %copy-start.6 = (bf16[1,32,4,8,256]{1,0,4,3,2:T(2,128)(2,1)S(1)}, bf16[1,32,4,8,256]{1,0,4,3,2:T(2,128)(2,1)}, u32[]{:S(2)}) copy-start(bf16[1,32,4,8,256]{1,0,4,3,2:T(2,128)(2,1)} %copy.368) | copy-start | bytes 1572868
  478.1 31.1 %copy-start.23 = (bf16[1,32,2,8,256]{1,0,4,3,2:T(2,128)(2,1)S(1)}, bf16[1,32,2,8,256]{1,0,4,3,2:T(2,128)(2,1)}, u32[]{:S(2)}) copy-start(bf16[1,32,2,8,256]{1,0,4,3,2:T(2,128)(2,1)} %copy.369) | copy-start | bytes 786436
  478.1 31.2 %copy-start.35 = (f32[32,32,3,3,3]{0,1,4,3,2:T(8,128)S(1)}, f32[32,32,3,3,3]{0,1,4,3,2:T(8,128)}, u32[]{:S(2)}) copy-start(f32[32,32,3,3,3]{0,1,4,3,2:T(8,128)} %fusion.179) | copy-start | bytes 331780
  478.1 31.2 %copy-start.36 = (f32[32,32,3,3,3]{0,1,4,3,2:T(8,128)S(1)}, f32[32,32,3,3,3]{0,1,4,3,2:T(8,128)}, u32[]{:S(2)}) copy-start(f32[32,32,3,3,3]{0,1,4,3,2:T(8,128)} %fusion.180) | copy-start | bytes 331780
  478.1 31.2 %copy-start.37 = (f32[32,32,3,3,3]{0,1,4,3,2:T(8,128)S(1)}, f32[32,32,3,3,3]{0,1,4,3,2:T(8,128)}, u32[]{:S(2)}) copy-start(f32[32,32,3,3,3]{0,1,4,3,2:T(8,128)} %fusion.181) | copy-start | bytes 331780
  698.6 2.3 copy-start.34
  (3 other events, 2.6 us)
Sparse Core Ops, SparseCore 0:
  540.0 142.3 all-reduce.1
where the time goes:
time: 722 us; the launch traced here: 714 us
  matrix products  214 us (30%)
  local copies, waits for them, and re-layouts  188 us (26%)
  waiting for transfers between devices  175 us (24%)
  starting transfers between devices  79.4 us (11%)
  other arithmetic  41.6 us (6%)
  between operations  15.2 us (2%)
    transpose x5, matrix products, kernel_grad(): return jnp.transpose(raw_grad, (1, 0, 2, 3, 4))  154 us
    psum x1, waiting for transfers between devices, body(): summed = lax.psum(local_grads, ('lat', 'dp'))  142 us
    conv_general_dilated x50, local copies, waits for them, and re-layouts, apply_conv(): lax.conv_general_dilated(padded, kernel, (1, 1, 1), ((0, 0), (1, 1), (1,...  108 us
    conv_general_dilated x10, matrix products, apply_conv(): lax.conv_general_dilated(padded, kernel, (1, 1, 1), ((0, 0), (1, 1), (1,...  60 us
    ppermute x10, starting transfers between devices, padded_2(): lax.ppermute(lax.slice_in_dim(block, block.shape[dim] - width, None, axis...  53.2 us
    concatenate x15, local copies, waits for them, and re-layouts, padded_2(): block = jnp.concatenate([low, block, high], axis=dim)  27.8 us
    mul x10, local copies, waits for them, and re-layouts, slope(): return sigmoid_val * (1.0 + pre_act * (1.0 - sigmoid_val))  23.8 us
    ppermute x10, waiting for transfers between devices, padded_2(): lax.ppermute(lax.slice_in_dim(block, block.shape[dim] - width, None, axis...  17.9 us
  transfers between devices with their start and end apart: 29, of which 17 were waited for; matrix products, arithmetic and copies ran while one was open for 30% of the time, Pallas kernels for 0%

commit v1 on v0

v1 whole, which is shorter than its diff:
```python
import functools

import jax
import jax.numpy as jnp
from jax import lax
from jax.experimental import pallas as pl
from jax.experimental.pallas import tpu as pltpu
from jax.sharding import PartitionSpec as P

AXES = ("section", "lat", "dp")
BF = jnp.bfloat16
F32 = jnp.float32
VMEM_BYTES = 60 * 1024 * 1024


def permute(value, move):
    sizes = [lax.axis_size(a) for a in AXES]
    pairs = []
    for s in range(sizes[0]):
        for l in range(sizes[1]):
            for d in range(sizes[2]):
                target = move(s, l, d)
                if target is None or not 0 <= target[1] < sizes[1]:
                    continue
                source_id = (s * sizes[1] + l) * sizes[2] + d
                target_id = (target[0] * sizes[1] + target[1]) * sizes[2] + target[2]
                pairs.append((source_id, target_id))
    return lax.ppermute(value, AXES, pairs)


def lat_move(even, odd):
    return lambda s, l, d: (s, l + (odd if l % 2 else even), d)


PARTNER = lat_move(1, -1)
NEAR_CROSS = lat_move(-1, 1)
NEAR_SAME = lat_move(-2, 2)
FAR_SAME = lat_move(2, -2)
FAR_CROSS = lat_move(3, -3)


def other_section(s, l, d):
    return (1 - s, l, d)


def ring(axis, step):
    def move(s, l, d):
        at = [l // 8, (l // 2) % 4, d * 2 + l % 2]
        at[axis] = (at[axis] + step) % 4
        return (s, at[0] * 8 + at[1] * 2 + at[2] % 2, at[2] // 2)

    return move


def to_field(field, cross, flip):
    def move(s, l, d):
        if (s != field) != cross:
            return None
        return (field, l ^ 1 if flip else l, d)

    return move


def load_cell(ref, cell):
    part = ref[:, cell]
    return part.astype(F32).reshape(256, 256)


def put_stack(ref, at, value):
    lane = lax.broadcasted_iota(jnp.int32, (256, 256), 1)
    before = jnp.where(lane == 0, 0.0, pltpu.roll(value, 1, 1))
    after = jnp.where(lane == 255, 0.0, pltpu.roll(value, 255, 1))
    ref[at, 0:256] = before.astype(BF)
    ref[at, 256:512] = value.astype(BF)
    ref[at, 512:768] = after.astype(BF)


def conv_cell(mat, block, slices):
    total = None
    for p in range(3):
        term = jnp.dot(mat[block, p], slices[p], preferred_element_type=F32)
        total = term if total is None else total + term
    return total


def round_bf(value):
    return value.astype(BF).astype(F32)


def slope(value):
    sig = jax.nn.sigmoid(value)
    return sig * (1.0 + value * (1.0 - sig))


def band_kernel(w_ref, wt_ref, out_ref):
    row = lax.broadcasted_iota(jnp.int32, (256, 256), 0) % 8
    lane = lax.broadcasted_iota(jnp.int32, (256, 256), 1) % 8
    gap = lane - row
    spread = jnp.where(
        lax.broadcasted_iota(jnp.int32, (32, 256), 1) // 8
        == lax.broadcasted_iota(jnp.int32, (32, 256), 0),
        1.0,
        0.0,
    ).astype(BF)
    tall = jnp.where(
        lax.broadcasted_iota(jnp.int32, (256, 32), 0) // 8
        == lax.broadcasted_iota(jnp.int32, (256, 32), 1),
        1.0,
        0.0,
    ).astype(BF)
    for block in range(2):
        for back in range(2):
            src = wt_ref if back else w_ref
            wide = jnp.dot(
                src[block].reshape(864, 32), spread, preferred_element_type=F32
            ).astype(BF)
            for p in range(3):
                for r in range(3):
                    mat = jnp.zeros((256, 256), F32)
                    for q in range(3):
                        n = (p * 3 + q) * 3 + r
                        if back:
                            n = 26 - n
                        full = jnp.dot(
                            tall, wide[32 * n : 32 * n + 32], preferred_element_type=F32
                        )
                        mat = jnp.where(gap == q - 1, full, mat)
                    out_ref[2 * block + back, p, :, 256 * r : 256 * r + 256] = mat.astype(BF)


def make_bands(w, wt):
    return pl.pallas_call(
        band_kernel,
        out_shape=jax.ShapeDtypeStruct((4, 3, 256, 768), BF),
        compiler_params=pltpu.CompilerParams(vmem_limit_bytes=VMEM_BYTES),
        name="bands",
    )(w, wt)


def valid_cell(at, pair, pairs):
    if at < 0:
        return pair > 0
    if at >= 4:
        return pair < pairs - 1
    return None


def masked(value, at, pair, pairs):
    ok = valid_cell(at, pair, pairs)
    return value if ok is None else jnp.where(ok, value, 0.0)


def pick_slab(refs, z):
    own, partner, nc, ns, fc, fs = refs
    return [(fs, fc), (nc, ns), (own, partner), (partner, own), (ns, nc), (fc, fs)]


def forward_kernel(pairs, pos_ref, own, partner, nc, ns, fc, fs, mat,
                   xv_ref, xm_ref, pre0_ref, pre1_ref, top_own, top_oth, xv_s, xm_s):
    z = pos_ref[0]
    pair = pos_ref[1]
    even = z == 0
    slabs = pick_slab((own, partner, nc, ns, fc, fs), z)

    def xv(a):
        return (xv_ref, a + 1) if -1 <= a < 5 else (xv_s, a + 4 if a < -1 else a - 2)

    def xm(a):
        return (xm_ref, a + 1) if -1 <= a < 5 else (xm_s, a + 3 if a < -1 else a - 3)

    for a in range(-4, 8):
        j = a + 4
        first, second = slabs[j // 2]
        value = jnp.where(even, load_cell(first, j % 2), load_cell(second, j % 2))
        ref, at = xv(a)
        put_stack(ref, at, value)
    for a in range(-3, 7):
        near = [xv(a + p - 1) for p in range(3)]
        pre = conv_cell(mat, 0, [ref[at] for ref, at in near])
        if -1 <= a < 5:
            pre0_ref[a + 1] = pre
        field = near[1][0][near[1][1], 256:512].astype(F32)
        mid = round_bf(field + pre * jax.nn.sigmoid(pre))
        ref, at = xm(a)
        put_stack(ref, at, masked(mid, a, pair, pairs))
    for a in range(-2, 6):
        near = [xm(a + p - 1) for p in range(3)]
        pre = conv_cell(mat, 2, [ref[at] for ref, at in near])
        pre1_ref[a + 2] = pre
        if 0 <= a < 4:
            mid = near[1][0][near[1][1], 256:512].astype(F32)
            top = (mid + pre * jax.nn.sigmoid(pre)).reshape(32, 8, 256).astype(BF)
            mine = even if a < 2 else jnp.logical_not(even)

            @pl.when(mine)
            def _():
                top_own[:, a % 2] = top

            @pl.when(jnp.logical_not(mine))
            def _():
                top_oth[:, a % 2] = top


VM = pl.BlockSpec(memory_space=pltpu.MemorySpace.VMEM)
SM = pl.BlockSpec(memory_space=pltpu.MemorySpace.SMEM)
SLAB = jax.ShapeDtypeStruct((32, 2, 8, 256), BF)
STACK = jax.ShapeDtypeStruct((6, 768, 256), BF)


def run_forward(pairs, pos, slabs, mats):
    return pl.pallas_call(
        functools.partial(forward_kernel, pairs),
        in_specs=[SM] + [VM] * 7,
        out_specs=[VM] * 6,
        out_shape=[
            STACK,
            STACK,
            jax.ShapeDtypeStruct((6, 256, 256), F32),
            jax.ShapeDtypeStruct((8, 256, 256), F32),
            SLAB,
            SLAB,
        ],
        scratch_shapes=[pltpu.VMEM((6, 768, 256), BF), pltpu.VMEM((4, 768, 256), BF)],
        compiler_params=pltpu.CompilerParams(vmem_limit_bytes=VMEM_BYTES),
        name="forward",
    )(pos, *slabs, mats)


def kernel_grad(delta_ref, x_ref, store):
    delta = jnp.concatenate([delta_ref(a) for a in range(4)], axis=1)
    row = lax.broadcasted_iota(jnp.int32, (256, 256), 0) % 8
    lane = lax.broadcasted_iota(jnp.int32, (256, 256), 1) % 8
    gap = lane - row
    fold_row = lax.broadcasted_iota(jnp.int32, (2048, 128), 0)
    fold_lane = lax.broadcasted_iota(jnp.int32, (2048, 128), 1)
    fold = jnp.where((fold_row % 1024) // 8 == fold_lane, 1.0, 0.0).astype(BF)
    parts = {}
    for p in range(3):
        field = jnp.concatenate([x_ref[a + p] for a in range(4)], axis=1)
        full = lax.dot_general(
            delta, field, (((1,), (1,)), ((), ())), preferred_element_type=F32
        )
        for r in range(3):
            piece = full[:, 256 * r : 256 * r + 256]
            for q in range(3):
                parts[(p * 3 + q) * 3 + r] = jnp.where(gap == q - 1, piece, 0.0)
        for u in range(7):
            members = [n for n in range(4 * u, 4 * u + 4) if n < 27]
            if not all(n in parts for n in members) or max(members) < 9 * p:
                continue
            high = []
            low = []
            for n in range(4 * u, 4 * u + 4):
                if n < 27:
                    part = parts[n]
                    top = part.astype(BF)
                    high.append(top)
                    low.append((part - top.astype(F32)).astype(BF))
                else:
                    high.append(jnp.zeros((256, 256), BF))
                    low.append(jnp.zeros((256, 256), BF))
            summed = jnp.dot(
                jnp.concatenate(high + low, axis=1), fold, preferred_element_type=F32
            )
            store(u, summed.reshape(32, 8, 128).sum(axis=1))


def backward_kernel(pairs, pos_ref, own, partner, nc, ns, mat, xv_ref, xm_ref, pre0_ref,
                    pre1_ref, xd0_ref, bm_ref, keep_ref, send_ref, xd1_s, bmh_s, cot_s):
    z = pos_ref[0]
    pair = pos_ref[1]
    even = z == 0
    zero_section = pos_ref[2] == 0
    slabs = [(nc, ns), (own, partner), (partner, own), (ns, nc)]
    for a in range(-2, 6):
        j = a + 2
        first, second = slabs[j // 2]
        cot = jnp.where(even, load_cell(first, j % 2), load_cell(second, j % 2))
        put_stack(xd1_s, j, round_bf(cot * slope(pre1_ref[j])))
        if -1 <= a < 5:
            cot_s[a + 1] = cot
    for a in range(-1, 5):
        pre = conv_cell(mat, 3, [xd1_s[a + 2 + p - 1] for p in range(3)])
        back = round_bf(cot_s[a + 1] + pre)
        if 0 <= a < 4:
            bm_ref[a] = back.astype(BF)
        delta = round_bf(back * slope(pre0_ref[a + 1]))
        put_stack(xd0_ref, a + 1, masked(delta, a, pair, pairs))

    def store_zero(u, value):
        rows = slice(32 * u, 32 * u + 32)

        @pl.when(zero_section)
        def _():
            keep_ref[rows] = value

        @pl.when(jnp.logical_not(zero_section))
        def _():
            send_ref[rows] = value

    def store_one(u, value):
        rows = slice(32 * u, 32 * u + 32)

        @pl.when(zero_section)
        def _():
            send_ref[rows] = value

        @pl.when(jnp.logical_not(zero_section))
        def _():
            keep_ref[rows] = value

    kernel_grad(lambda a: xd0_ref[a + 1, 256:512], xv_ref, store_zero)
    kernel_grad(lambda a: xd1_s[a + 2, 256:512], xm_ref, store_one)


def run_backward(pairs, pos, slabs, mats, xv, xm, pre0, pre1):
    grad = jax.ShapeDtypeStruct((224, 128), F32)
    return pl.pallas_call(
        functools.partial(backward_kernel, pairs),
        in_specs=[SM] + [VM] * 9,
        out_specs=[VM] * 4,
        out_shape=[STACK, jax.ShapeDtypeStruct((4, 256, 256), BF), grad, grad],
        scratch_shapes=[
            pltpu.VMEM((8, 768, 256), BF),
            pltpu.VMEM((1, 8, 128), F32),
            pltpu.VMEM((6, 256, 256), F32),
        ],
        compiler_params=pltpu.CompilerParams(vmem_limit_bytes=VMEM_BYTES),
        name="backward",
    )(pos, *slabs, mats, xv, xm, pre0, pre1)


def last_kernel(pos_ref, xd0_ref, bm_ref, mat, out_own, out_oth):
    even = pos_ref[0] == 0
    for a in range(4):
        pre = conv_cell(mat, 1, [xd0_ref[a + p] for p in range(3)])
        out = (bm_ref[a].astype(F32) + pre).reshape(32, 8, 256).astype(BF)
        mine = even if a < 2 else jnp.logical_not(even)

        @pl.when(mine)
        def _():
            out_own[:, a % 2] = out

        @pl.when(jnp.logical_not(mine))
        def _():
            out_oth[:, a % 2] = out


def run_last(pos, xd0, bm, mats):
    return pl.pallas_call(
        last_kernel,
        in_specs=[SM] + [VM] * 3,
        out_specs=[VM] * 2,
        out_shape=[SLAB, SLAB],
        compiler_params=pltpu.CompilerParams(vmem_limit_bytes=VMEM_BYTES),
        name="last",
    )(pos, xd0, bm, mats)


def gather_kernel(pos_ref, *refs):
    pieces, (out_ref, sems) = refs[:8], refs[8:]
    z = pos_ref[0]
    s = pos_ref[2]
    for field in range(2):
        @pl.when(s == field)
        def _():
            copies = []
            for n in range(4):
                clip = 2 * (s ^ (n // 2)) + (z ^ (n % 2))
                copies.append(
                    pltpu.make_async_copy(
                        pieces[4 * field + n], out_ref.at[clip], sems.at[n]
                    )
                )
            for copy in copies:
                copy.start()
            for copy in copies:
                copy.wait()


def run_gather(pos, pieces):
    hbm = pl.BlockSpec(memory_space=pl.ANY)
    return pl.pallas_call(
        gather_kernel,
        in_specs=[SM] + [hbm] * 8,
        out_specs=hbm,
        out_shape=jax.ShapeDtypeStruct((4, 32, 2, 8, 256), BF),
        scratch_shapes=[pltpu.SemaphoreType.DMA((4,))],
        name="gather",
    )(pos, *pieces)


def unfold_kernel(in_ref, out_ref):
    for n in range(27):
        u, g = divmod(n, 4)
        out_ref[n] = in_ref[32 * u : 32 * u + 32, 32 * g : 32 * g + 32]


def run_unfold(grads):
    return pl.pallas_call(
        unfold_kernel,
        out_shape=jax.ShapeDtypeStruct((27, 32, 32), F32),
        name="unfold",
    )(grads)


def body(volume, cotangent, weights):
    s = lax.axis_index("section")
    l = lax.axis_index("lat")
    pairs = lax.axis_size("lat") // 2
    z = l % 2
    pos = jnp.stack([z, l // 2, s]).astype(jnp.int32)

    def clip(array, at):
        return lax.dynamic_index_in_dim(array, at, 0, keepdims=False)

    same = 2 * s + z
    cross = 2 * s + (1 - z)
    mine = jnp.transpose(weights[0], (2, 3, 4, 0, 1)).reshape(27, 32, 32)
    others = permute(mine, other_section)
    v_same, v_cross = clip(volume, same), clip(volume, cross)
    v_slabs = [
        v_same,
        permute(v_cross, PARTNER),
        permute(v_cross, NEAR_CROSS),
        permute(v_same, NEAR_SAME),
        permute(v_cross, FAR_CROSS),
        permute(v_same, FAR_SAME),
    ]
    c_same, c_cross = clip(cotangent, same), clip(cotangent, cross)
    c_slabs = [
        c_same,
        permute(c_cross, PARTNER),
        permute(c_cross, NEAR_CROSS),
        permute(c_same, NEAR_SAME),
    ]
    both = jnp.where(
        s == 0, jnp.stack([mine, others]), jnp.stack([others, mine])
    )
    mats = make_bands(both, jnp.swapaxes(both, 2, 3))
    xv, xm, pre0, pre1, top_own, top_oth = run_forward(pairs, pos, v_slabs, mats)
    top_pieces = [
        top_own,
        permute(top_oth, to_field(1, False, True)),
        permute(top_own, to_field(1, True, False)),
        permute(top_oth, to_field(1, True, True)),
    ]
    xd0, bm, keep, send = run_backward(pairs, pos, c_slabs, mats, xv, xm, pre0, pre1)
    out_own, out_oth = run_last(pos, xd0, bm, mats)
    out_pieces = [
        out_own,
        permute(out_oth, to_field(0, False, True)),
        permute(out_own, to_field(0, True, False)),
        permute(out_oth, to_field(0, True, True)),
    ]
    total = keep + permute(send, other_section)
    for axis in (2, 1, 0):
        total = (total + permute(total, ring(axis, 2))) + (
            permute(total, ring(axis, 1)) + permute(total, ring(axis, 3))
        )
    field = run_gather(pos, out_pieces + top_pieces)
    grads = run_unfold(total).reshape(3, 3, 3, 32, 32)
    return (field[None], jnp.transpose(grads, (3, 4, 0, 1, 2))[None])


def solution(mesh):
    return jax.shard_map(
        body,
        mesh=mesh,
        in_specs=(
            P("dp", None, "lat", None, None),
            P("dp", None, "lat", None, None),
            P("section", None, None, None, None, None),
        ),
        out_specs=(
            P("section", "dp", None, "lat", None, None),
            P("section", None, None, None, None, None),
        ),
        check_vma=False,
    )
```

time: 722 us -> 154 us (0.21)
  matrix products: 214 us -> 0 us
  local copies, waits for them, and re-layouts: 188 us -> 7.77 us
  waiting for transfers between devices: 175 us -> 2.73 us
  Pallas kernels: 0 us -> 84 us
  other arithmetic: 41.6 us -> 3.37 us
  starting transfers between devices: 79.4 us -> 53.4 us
  between operations: 15.2 us -> 1.11 us
    transpose x5 -> x0, matrix products: 154 us -> none  [kernel_grad(): return jnp.transpose(raw_grad, (1, 0, 2, 3, 4))]
    psum x1 -> x0, waiting for transfers between devices: 142 us -> none  [body(): summed = lax.psum(local_grads, ('lat', 'dp'))]
    conv_general_dilated x50 -> x0, local copies, waits for them, and re-layouts: 108 us -> none  [apply_conv(): lax.conv_general_dilated(padded, kernel, (1, 1, 1), ((0, 0), (1, 1), (1,...]
    pallas_call x0 -> x6, Pallas kernels: none -> 84 us  [the longest x1 33.6 us: run_gather(): pl.pallas_call(gather_kernel, in_specs=[SM] + [hbm] * 8, out_specs=hbm, o...]
    conv_general_dilated x10 -> x0, matrix products: 60 us -> none  [apply_conv(): lax.conv_general_dilated(padded, kernel, (1, 1, 1), ((0, 0), (1, 1), (1,...]
    mul x20 -> x0, local copies, waits for them, and re-layouts: 36.4 us -> none  [the longest x10 23.8 us: slope(): return sigmoid_val * (1.0 + pre_act * (1.0 - sigmoid_val))]
    ppermute x28 -> x25, waiting for transfers between devices: 32.9 us -> 2.73 us  [permute(): return lax.ppermute(value, AXES, pairs)]
    concatenate x15 -> x0, local copies, waits for them, and re-layouts: 27.8 us -> none  [padded_2(): block = jnp.concatenate([low, block, high], axis=dim)]
  transfers between devices with their start and end apart: 29 -> 25, of which waited for: 17 -> 3; matrix products, arithmetic and copies ran while one was open for 30% -> 3% of each run, Pallas kernels for 0% -> 41%
where the time goes in v1:
time: 154 us; the launch traced here: 152 us
  Pallas kernels  84 us (55%)
  starting transfers between devices  53.4 us (35%)
  local copies, waits for them, and re-layouts  7.77 us (5%)
  other arithmetic  3.37 us (2%)
  waiting for transfers between devices  2.73 us (2%)
    ppermute x25, starting transfers between devices, permute(): return lax.ppermute(value, AXES, pairs)  53.4 us
    pallas_call x1, Pallas kernels, run_gather(): pl.pallas_call(gather_kernel, in_specs=[SM] + [hbm] * 8, out_specs=hbm, o...  33.6 us
    pallas_call x1, Pallas kernels, run_backward(): pl.pallas_call(functools.partial(backward_kernel, pairs), in_specs=[SM] +...  19.7 us
    pallas_call x1, Pallas kernels, run_forward(): pl.pallas_call(functools.partial(forward_kernel, pairs), in_specs=[SM] +...  13.4 us
    pallas_call x1, Pallas kernels, make_bands(): pl.pallas_call(band_kernel, out_shape=jax.ShapeDtypeStruct((4, 3, 256, 76...  8.48 us
    pallas_call x1, Pallas kernels, run_last(): pl.pallas_call(last_kernel, in_specs=[SM] + [VM] * 3, out_specs=[VM] * 2,...  7.13 us
    unnamed x34, local copies, waits for them, and re-layouts  3.58 us
  transfers between devices with their start and end apart: 25, of which 3 were waited for; matrix products, arithmetic and copies ran while one was open for 3% of the time, Pallas kernels for 41%

profile of v1, /device:TPU:0, one launch (start us, length us, event | category | flops | bytes accessed | tf_op | source)
XLA Modules:
  0.0 152.4 jit_solution(15319914949621616530)
XLA Ops:
  0.7 1.1 dynamic-slice_bitcast_fusion
  1.7 5.0 %collective-permute-start.7 = (bf16[32,2,8,256]{3,2,1,0:T(8,128)(2,1)S(1)}, bf16[32,2,8,256]{3,2,1,0:T(8,128)(2,1)S(1)}, u32[]{:S(2)}, u32[]{:S(2)}) collective-permute-start(bf16[32,2,8,256]{3,2,1,0:T(8,128)(2,1)S(1)} %get-tuple-element.26), channel_id=1, source_target_pairs={{0,6},{1,7},{4,10},{5,11},{6,0},{7,1},{8,14},{9,15},{10,4},{11,5},... | collective-permute-start | bytes 786440 | tf_op jit(solution)/shard_map/ppermute | solution.py:28
  6.7 0.7 collective-permute-start.5
  7.4 4.3 %collective-permute-start.4 = (bf16[32,2,8,256]{3,2,1,0:T(8,128)(2,1)S(1)}, bf16[32,2,8,256]{3,2,1,0:T(8,128)(2,1)S(1)}, u32[]{:S(2)}, u32[]{:S(2)}) collective-permute-start(bf16[32,2,8,256]{3,2,1,0:T(8,128)(2,1)S(1)} %get-tuple-element.26), channel_id=1, source_target_pairs={{0,2},{1,3},{2,0},{3,1},{4,6},{5,7},{6,4},{7,5},{8,10},{9,11},{10,... | collective-permute-start | bytes 786440 | tf_op jit(solution)/shard_map/ppermute | solution.py:28
  11.7 1.1 copy.5
  12.8 0.1 collective-permute-start.3
  12.9 3.2 %collective-permute-start.8 = (bf16[32,2,8,256]{3,2,1,0:T(8,128)(2,1)S(1)}, bf16[32,2,8,256]{3,2,1,0:T(8,128)(2,1)S(1)}, u32[]{:S(2)}, u32[]{:S(2)}) collective-permute-start(bf16[32,2,8,256]{3,2,1,0:T(8,128)(2,1)S(1)} %get-tuple-element.27.own), channel_id=1, source_target_pairs={{0,4},{1,5},{4,8},{5,9},{6,2},{7,3},{8,12},{9,13},{10,6},{11,7},{1... | collective-permute-start | bytes 786440 | tf_op jit(solution)/shard_map/ppermute | solution.py:28
  16.1 1.1 dynamic-slice_bitcast_fusion.2
  17.2 0.0 collective-permute-done.3
  17.2 1.3 collective-permute-start.6
  18.5 0.0 collective-permute-done.7.fc
  18.6 0.7 collective-permute-start.1
  19.2 0.0 collective-permute-done.5.nc
  19.3 5.4 %collective-permute-start = (bf16[32,2,8,256]{3,2,1,0:T(8,128)(2,1)S(1)}, bf16[32,2,8,256]{3,2,1,0:T(8,128)(2,1)S(1)}, u32[]{:S(2)}, u32[]{:S(2)}) collective-permute-start(bf16[32,2,8,256]{3,2,1,0:T(8,128)(2,1)S(1)} %get-tuple-element.28), channel_id=1, source_target_pairs={{0,2},{1,3},{2,0},{3,1},{4,6},{5,7},{6,4},{7,5},{8,10},{9,11},{10,... | collective-permute-start | bytes 786440 | tf_op jit(solution)/shard_map/ppermute | solution.py:28
  24.7 0.0 collective-permute-done.4.partner
  24.7 1.3 collective-permute-start.2
  26.0 0.7 pad_add_fusion.pos_ref
  26.6 0.2 maximum_select_fusion
  26.8 1.0 copy.7.w_ref
  27.8 0.9 fusion.wt_ref
  28.7 8.5 %bands.1.mat = bf16[4,3,256,768]{3,2,1,0:T(8,128)(2,1)} custom-call(bf16[2,27,32,32]{3,2,1,0:T(8,128)(2,1)} %copy.7.w_ref, bf16[2,27,32,32]{3,2,1,0:T(8,128)(2,1)} %fusion.wt_ref), custom_call_target="tpu_custom_call" | custom-call | tf_op jit(solution)/shard_map/bands/pallas_call | solution.py:132
  37.2 0.0 collective-permute-done.8.fs
  37.2 0.0 copy-start.5
  37.2 0.0 collective-permute-done.6.ns
  37.2 0.7 copy-done.5
  37.9 0.7 copy-done.8
  38.6 13.4 %forward.1 = (bf16[6,768,256]{2,1,0:T(8,128)(2,1)}, bf16[6,768,256]{2,1,0:T(8,128)(2,1)}, f32[6,256,256]{2,1,0:T(8,128)}, f32[8,256,256]{2,1,0:T(8,128)}, bf16[3...) custom-call(s32[3]{0:T(128)} %pad_add_fusion.pos_ref, bf16[32,2,8,256]{3,2,1,0:T(8,128)(2,1)} %copy-done, ...), custom_call_target="tpu_custom_call" | custom-call | tf_op jit(solution)/shard_map/forward/pallas_call | solution.py:211
  52.0 0.0 collective-permute-done.1.nc
  52.0 0.0 collective-permute-done.partner
  52.0 0.0 copy-start.7
  52.0 0.0 collective-permute-done.2.ns
  52.0 0.7 copy-done.6
  52.7 0.1 copy-done.7
  52.8 19.7 %backward.1 = (bf16[6,768,256]{2,1,0:T(8,128)(2,1)}, bf16[4,256,256]{2,1,0:T(8,128)(2,1)}, f32[224,128]{1,0:T(8,128)}, f32[224,128]{1,0:T(8,128)}) custom-call(s32[3]{0:T(128)} %pad_add_fusion.pos_ref, bf16[32,2,8,256]{3,2,1,0:T(8,128)(2,1)} %copy-done.1, bf16[32,2,8,256]{3,2,1,0:T(8,128)(2,1)} %copy-done.7, bf16[32,2,8,256]{3,2,1,0:T(8,128)(2,1)} %copy-done.6, ...), custom_call_target="tpu_custom_call" | custom-call | tf_op jit(solution)/shard_map/backward/pallas_call | solution.py:318
  72.4 1.5 %collective-permute-done.15 = f32[224,128]{1,0:T(8,128)S(1)} collective-permute-done((f32[224,128]{1,0:T(8,128)}, f32[224,128]{1,0:T(8,128)S(1)}, u32[]{:S(2)}, u32[]{:S(2)}) %collective-permute-start.15) | collective-permute-done | bytes 114720 | tf_op jit(solution)/shard_map/ppermute | solution.py:28
  74.0 0.9 add.55
  74.9 6.2 %collective-permute-start.18 = (f32[224,128]{1,0:T(8,128)S(1)}, f32[224,128]{1,0:T(8,128)S(1)}, u32[]{:S(2)}, u32[]{:S(2)}) collective-permute-start(f32[224,128]{1,0:T(8,128)S(1)} %add.55), channel_id=1, source_target_pairs={{0,3},{1,2},{2,0},{3,1},{4,7},{5,6},{6,4},{7,5},{8,11},{9,10},{10,... | collective-permute-start | bytes 344072 | tf_op jit(solution)/shard_map/ppermute | solution.py:28
  81.1 1.5 %collective-permute-start.16 = (f32[224,128]{1,0:T(8,128)S(1)}, f32[224,128]{1,0:T(8,128)S(1)}, u32[]{:S(2)}, u32[]{:S(2)}) collective-permute-start(f32[224,128]{1,0:T(8,128)S(1)} %add.55), channel_id=1, source_target_pairs={{0,1},{1,0},{2,3},{3,2},{4,5},{5,4},{6,7},{7,6},{8,9},{9,8},{10,11... | collective-permute-start | bytes 344072 | tf_op jit(solution)/shard_map/ppermute | solution.py:28
  82.7 7.1 %last.1 = (bf16[32,2,8,256]{3,2,1,0:T(8,128)(2,1)}, bf16[32,2,8,256]{3,2,1,0:T(8,128)(2,1)}) custom-call(s32[3]{0:T(128)} %pad_add_fusion.pos_ref, bf16[6,768,256]{2,1,0:T(8,128)(2,1)} %get-tuple-element.18.xd0_ref, bf16[4,256,256]{2,1,0:T(8,128)(2,1)} %get-tuple-element.19.bm_ref, bf16[4,3,256,768]{3,2,1,0:T(8,128)(2,1)} %bands.1.mat), custom_call_target="tpu_custom_call" | custom-call | tf_op jit(solution)/shard_map/last/pallas_call | solution.py:350
  89.8 1.3 collective-permute-start.10
  91.1 0.0 collective-permute-done.18
  91.2 4.2 %collective-permute-start.21 = (f32[224,128]{1,0:T(8,128)S(1)}, f32[224,128]{1,0:T(8,128)S(1)}, u32[]{:S(2)}, u32[]{:S(2)}) collective-permute-start(f32[224,128]{1,0:T(8,128)S(1)} %add_add_fusion.2), channel_id=1, source_target_pairs={{0,12},{1,13},{2,14},{3,15},{4,0},{5,1},{6,2},{7,3},{8,4},{9,5},{1... | collective-permute-start | bytes 344072 | tf_op jit(solution)/shard_map/ppermute | solution.py:28
  95.3 0.0 collective-permute-start.20
  95.3 1.5 %collective-permute-start.19 = (f32[224,128]{1,0:T(8,128)S(1)}, f32[224,128]{1,0:T(8,128)S(1)}, u32[]{:S(2)}, u32[]{:S(2)}) collective-permute-start(f32[224,128]{1,0:T(8,128)S(1)} %add_add_fusion.2), channel_id=1, source_target_pairs={{0,8},{1,9},{2,10},{3,11},{4,12},{5,13},{6,14},{7,15},{8,0},{9,1},... | collective-permute-start | bytes 344072 | tf_op jit(solution)/shard_map/ppermute | solution.py:28
  96.9 1.3 collective-permute-start.11
  98.2 4.5 %collective-permute-start.9 = (bf16[32,2,8,256]{3,2,1,0:T(8,128)(2,1)}, bf16[32,2,8,256]{3,2,1,0:T(8,128)(2,1)S(1)}, u32[]{:S(2)}, u32[]{:S(2)}) collective-permute-start(bf16[32,2,8,256]{3,2,1,0:T(8,128)(2,1)} %get-tuple-element.21), channel_id=1, source_target_pairs={{0,2},{1,3},{2,0},{3,1},{4,6},{5,7},{6,4},{7,5},{8,10},{9,11},{10,... | collective-permute-start | bytes 786440 | tf_op jit(solution)/shard_map/ppermute | solution.py:28
  102.7 0.0 collective-permute-done.21
  102.7 1.4 collective-permute-start.13
  104.1 0.8 collective-permute-done.20
  104.9 4.1 %collective-permute-start.14 = (bf16[32,2,8,256]{3,2,1,0:T(8,128)(2,1)S(1)}, bf16[32,2,8,256]{3,2,1,0:T(8,128)(2,1)S(1)}, u32[]{:S(2)}, u32[]{:S(2)}) collective-permute-start(bf16[32,2,8,256]{3,2,1,0:T(8,128)(2,1)S(1)} %copy-done.16), channel_id=1, source_target_pairs={{0,66},{1,67},{2,64},{3,65},{4,70},{5,71},{6,68},{7,69},{8,74},{9,... | collective-permute-start | bytes 786440 | tf_op jit(solution)/shard_map/ppermute | solution.py:28
  109.0 0.7 collective-permute-start.12
  109.7 0.0 collective-permute-done.11.refs_3_
  109.7 0.1 collective-permute-start.24
  109.8 2.0 %collective-permute-start.23 = (f32[224,128]{1,0:T(8,128)S(1)}, f32[224,128]{1,0:T(8,128)S(1)}, u32[]{:S(2)}, u32[]{:S(2)}) collective-permute-start(f32[224,128]{1,0:T(8,128)S(1)} %add_add_fusion.1), channel_id=1, source_target_pairs={{0,16},{1,17},{2,18},{3,19},{4,20},{5,21},{6,22},{7,23},{8,24},{9,... | collective-permute-start | bytes 344072 | tf_op jit(solution)/shard_map/ppermute | solution.py:28
  111.8 0.0 collective-permute-done.13.refs_6_
  111.8 2.7 %collective-permute-start.22 = (f32[224,128]{1,0:T(8,128)S(1)}, f32[224,128]{1,0:T(8,128)S(1)}, u32[]{:S(2)}, u32[]{:S(2)}) collective-permute-start(f32[224,128]{1,0:T(8,128)S(1)} %add_add_fusion.1), channel_id=1, source_target_pairs={{0,32},{1,33},{2,34},{3,35},{4,36},{5,37},{6,38},{7,39},{8,40},{9,... | collective-permute-start | bytes 344072 | tf_op jit(solution)/shard_map/ppermute | solution.py:28
  114.6 0.3 collective-permute-done.14.refs_7_
  114.9 0.0 collective-permute-done.12.refs_5_
  115.0 0.7 copy-done.14
  115.6 0.7 copy-done.15
  116.4 33.6 %gather.1 = bf16[4,32,2,8,256]{4,3,2,1,0:T(8,128)(2,1)} custom-call(s32[3]{0:T(128)} %pad_add_fusion.pos_ref, bf16[32,2,8,256]{3,2,1,0:T(8,128)(2,1)} %get-tuple-element.20.refs_0_, bf16[32,2,8,256]{3,2,1,0:T(8,128)(2,1)} %copy-done.12, bf16[32,2,8,256]{3,2,1,0:T(8,128)(2,1)} %copy-done.10, bf16[32,2,8,256]{3,2,1,0:T(8,128)(2,1)} %copy-done.11, ...), custom_call_target="tpu_custom_call" | custom-call | tf_op jit(solution)/shard_map/gather/pallas_call | solution.py:383
  149.9 0.0 collective-permute-done.24
  150.0 0.7 add_add_fusion.in_ref
  150.6 1.8 %unfold.1 = f32[27,32,32]{2,1,0:T(8,128)} custom-call(f32[224,128]{1,0:T(8,128)} %add_add_fusion.in_ref), custom_call_target="tpu_custom_call" | custom-call | tf_op jit(solution)/shard_map/unfold/pallas_call | solution.py:400
  (37 shorter events, 0.1 us)
Async XLA Ops:
  1.7 35.4 %copy-start = (bf16[32,2,8,256]{3,2,1,0:T(8,128)(2,1)}, bf16[32,2,8,256]{3,2,1,0:T(8,128)(2,1)S(1)}, u32[]{:S(2)}) copy-start(bf16[32,2,8,256]{3,2,1,0:T(8,128)(2,1)S(1)} %get-tuple-element.27.own) | copy-start | bytes 786436
  1.7 16.8 %collective-permute-start.7 = (bf16[32,2,8,256]{3,2,1,0:T(8,128)(2,1)S(1)}, bf16[32,2,8,256]{3,2,1,0:T(8,128)(2,1)S(1)}, u32[]{:S(2)}, u32[]{:S(2)}) collective-permute-start(bf16[32,2,8,256]{3,2,1,0:T(8,128)(2,1)S(1)} %get-tuple-element.26), channel_id=1, source_target_pairs={{0,6},{1,7},{4,10},{5,11},{6,0},{7,1},{8,14},{9,15},{10,4},{11,5},... | collective-permute-start | bytes 786440 | tf_op jit(solution)/shard_map/ppermute | solution.py:28
  6.7 12.5 %collective-permute-start.5 = (bf16[32,2,8,256]{3,2,1,0:T(8,128)(2,1)S(1)}, bf16[32,2,8,256]{3,2,1,0:T(8,128)(2,1)S(1)}, u32[]{:S(2)}, u32[]{:S(2)}) collective-permute-start(bf16[32,2,8,256]{3,2,1,0:T(8,128)(2,1)S(1)} %get-tuple-element.26), channel_id=1, source_target_pairs={{2,4},{3,5},{4,2},{5,3},{6,8},{7,9},{8,6},{9,7},{10,12},{11,13},{1... | collective-permute-start | bytes 786440 | tf_op jit(solution)/shard_map/ppermute | solution.py:28
  7.4 17.3 %collective-permute-start.4 = (bf16[32,2,8,256]{3,2,1,0:T(8,128)(2,1)S(1)}, bf16[32,2,8,256]{3,2,1,0:T(8,128)(2,1)S(1)}, u32[]{:S(2)}, u32[]{:S(2)}) collective-permute-start(bf16[32,2,8,256]{3,2,1,0:T(8,128)(2,1)S(1)} %get-tuple-element.26), channel_id=1, source_target_pairs={{0,2},{1,3},{2,0},{3,1},{4,6},{5,7},{6,4},{7,5},{8,10},{9,11},{10,... | collective-permute-start | bytes 786440 | tf_op jit(solution)/shard_map/ppermute | solution.py:28
  12.8 4.4 %collective-permute-start.3 = (bf16[27,32,32]{1,2,0:T(8,128)(2,1)S(1)}, bf16[27,32,32]{1,2,0:T(8,128)(2,1)S(1)}, u32[]{:S(2)}, u32[]{:S(2)}) collective-permute-start(bf16[27,32,32]{1,2,0:T(8,128)(2,1)S(1)} %bitcast.25), channel_id=1, source_target_pairs={{0,64},{1,65},{2,66},{3,67},{4,68},{5,69},{6,70},{7,71},{8,72},{9,... | collective-permute-start | bytes 165896 | tf_op jit(solution)/shard_map/ppermute | solution.py:28
  12.9 24.3 %collective-permute-start.8 = (bf16[32,2,8,256]{3,2,1,0:T(8,128)(2,1)S(1)}, bf16[32,2,8,256]{3,2,1,0:T(8,128)(2,1)S(1)}, u32[]{:S(2)}, u32[]{:S(2)}) collective-permute-start(bf16[32,2,8,256]{3,2,1,0:T(8,128)(2,1)S(1)} %get-tuple-element.27.own), channel_id=1, source_target_pairs={{0,4},{1,5},{4,8},{5,9},{6,2},{7,3},{8,12},{9,13},{10,6},{11,7},{1... | collective-permute-start | bytes 786440 | tf_op jit(solution)/shard_map/ppermute | solution.py:28
  17.2 20.0 %copy-start.1 = (bf16[32,2,8,256]{3,2,1,0:T(8,128)(2,1)}, bf16[32,2,8,256]{3,2,1,0:T(8,128)(2,1)S(1)}, u32[]{:S(2)}) copy-start(bf16[32,2,8,256]{3,2,1,0:T(8,128)(2,1)S(1)} %get-tuple-element.29.own) | copy-start | bytes 786436
  17.2 20.0 %collective-permute-start.6 = (bf16[32,2,8,256]{3,2,1,0:T(8,128)(2,1)S(1)}, bf16[32,2,8,256]{3,2,1,0:T(8,128)(2,1)S(1)}, u32[]{:S(2)}, u32[]{:S(2)}) collective-permute-start(bf16[32,2,8,256]{3,2,1,0:T(8,128)(2,1)S(1)} %get-tuple-element.27.own), channel_id=1, source_target_pairs={{2,6},{3,7},{4,0},{5,1},{6,10},{7,11},{8,4},{9,5},{10,14},{11,15},... | collective-permute-start | bytes 786440 | tf_op jit(solution)/shard_map/ppermute | solution.py:28
  18.5 18.6 %copy-start.2 = (bf16[32,2,8,256]{3,2,1,0:T(8,128)(2,1)}, bf16[32,2,8,256]{3,2,1,0:T(8,128)(2,1)S(1)}, u32[]{:S(2)}) copy-start(bf16[32,2,8,256]{3,2,1,0:T(8,128)(2,1)S(1)} %collective-permute-done.7.fc) | copy-start | bytes 786436
  18.6 33.4 %collective-permute-start.1 = (bf16[32,2,8,256]{3,2,1,0:T(8,128)(2,1)S(1)}, bf16[32,2,8,256]{3,2,1,0:T(8,128)(2,1)S(1)}, u32[]{:S(2)}, u32[]{:S(2)}) collective-permute-start(bf16[32,2,8,256]{3,2,1,0:T(8,128)(2,1)S(1)} %get-tuple-element.28), channel_id=1, source_target_pairs={{2,4},{3,5},{4,2},{5,3},{6,8},{7,9},{8,6},{9,7},{10,12},{11,13},{1... | collective-permute-start | bytes 786440 | tf_op jit(solution)/shard_map/ppermute | solution.py:28
  19.2 17.9 %copy-start.3 = (bf16[32,2,8,256]{3,2,1,0:T(8,128)(2,1)}, bf16[32,2,8,256]{3,2,1,0:T(8,128)(2,1)S(1)}, u32[]{:S(2)}) copy-start(bf16[32,2,8,256]{3,2,1,0:T(8,128)(2,1)S(1)} %collective-permute-done.5.nc) | copy-start | bytes 786436
  19.3 32.7 %collective-permute-start = (bf16[32,2,8,256]{3,2,1,0:T(8,128)(2,1)S(1)}, bf16[32,2,8,256]{3,2,1,0:T(8,128)(2,1)S(1)}, u32[]{:S(2)}, u32[]{:S(2)}) collective-permute-start(bf16[32,2,8,256]{3,2,1,0:T(8,128)(2,1)S(1)} %get-tuple-element.28), channel_id=1, source_target_pairs={{0,2},{1,3},{2,0},{3,1},{4,6},{5,7},{6,4},{7,5},{8,10},{9,11},{10,... | collective-permute-start | bytes 786440 | tf_op jit(solution)/shard_map/ppermute | solution.py:28
  24.7 12.5 %copy-start.4 = (bf16[32,2,8,256]{3,2,1,0:T(8,128)(2,1)}, bf16[32,2,8,256]{3,2,1,0:T(8,128)(2,1)S(1)}, u32[]{:S(2)}) copy-start(bf16[32,2,8,256]{3,2,1,0:T(8,128)(2,1)S(1)} %collective-permute-done.4.partner) | copy-start | bytes 786436
  24.7 27.3 %collective-permute-start.2 = (bf16[32,2,8,256]{3,2,1,0:T(8,128)(2,1)S(1)}, bf16[32,2,8,256]{3,2,1,0:T(8,128)(2,1)}, u32[]{:S(2)}, u32[]{:S(2)}) collective-permute-start(bf16[32,2,8,256]{3,2,1,0:T(8,128)(2,1)S(1)} %get-tuple-element.29.own), channel_id=1, source_target_pairs={{2,6},{3,7},{4,0},{5,1},{6,10},{7,11},{8,4},{9,5},{10,14},{11,15},... | collective-permute-start | bytes 786440 | tf_op jit(solution)/shard_map/ppermute | solution.py:28
  37.2 0.7 copy-start.5
  37.9 0.7 copy-start.8
  52.0 0.7 copy-start.6
  52.0 0.8 copy-start.7
  72.4 1.5 %collective-permute-start.15 = (f32[224,128]{1,0:T(8,128)}, f32[224,128]{1,0:T(8,128)S(1)}, u32[]{:S(2)}, u32[]{:S(2)}) collective-permute-start(f32[224,128]{1,0:T(8,128)} %get-tuple-element.25), channel_id=1, source_target_pairs={{0,64},{1,65},{2,66},{3,67},{4,68},{5,69},{6,70},{7,71},{8,72},{9,... | collective-permute-start | bytes 344072 | tf_op jit(solution)/shard_map/ppermute | solution.py:28
  74.9 16.2 %collective-permute-start.18 = (f32[224,128]{1,0:T(8,128)S(1)}, f32[224,128]{1,0:T(8,128)S(1)}, u32[]{:S(2)}, u32[]{:S(2)}) collective-permute-start(f32[224,128]{1,0:T(8,128)S(1)} %add.55), channel_id=1, source_target_pairs={{0,3},{1,2},{2,0},{3,1},{4,7},{5,6},{6,4},{7,5},{8,11},{9,10},{10,... | collective-permute-start | bytes 344072 | tf_op jit(solution)/shard_map/ppermute | solution.py:28
  81.1 10.0 %collective-permute-start.17 = (f32[224,128]{1,0:T(8,128)S(1)}, f32[224,128]{1,0:T(8,128)S(1)}, u32[]{:S(2)}, u32[]{:S(2)}) collective-permute-start(f32[224,128]{1,0:T(8,128)S(1)} %add.55), channel_id=1, source_target_pairs={{0,2},{1,3},{2,1},{3,0},{4,6},{5,7},{6,5},{7,4},{8,10},{9,11},{10,... | collective-permute-start | bytes 344072 | tf_op jit(solution)/shard_map/ppermute | solution.py:28
  81.1 10.0 %collective-permute-start.16 = (f32[224,128]{1,0:T(8,128)S(1)}, f32[224,128]{1,0:T(8,128)S(1)}, u32[]{:S(2)}, u32[]{:S(2)}) collective-permute-start(f32[224,128]{1,0:T(8,128)S(1)} %add.55), channel_id=1, source_target_pairs={{0,1},{1,0},{2,3},{3,2},{4,5},{5,4},{6,7},{7,6},{8,9},{9,8},{10,11... | collective-permute-start | bytes 344072 | tf_op jit(solution)/shard_map/ppermute | solution.py:28
  82.7 20.0 %copy-start.9 = (bf16[32,2,8,256]{3,2,1,0:T(8,128)(2,1)S(1)}, bf16[32,2,8,256]{3,2,1,0:T(8,128)(2,1)}, u32[]{:S(2)}) copy-start(bf16[32,2,8,256]{3,2,1,0:T(8,128)(2,1)} %get-tuple-element.22.refs_4_) | copy-start | bytes 786436
  82.7 22.3 %copy-start.16 = (bf16[32,2,8,256]{3,2,1,0:T(8,128)(2,1)S(1)}, bf16[32,2,8,256]{3,2,1,0:T(8,128)(2,1)}, u32[]{:S(2)}) copy-start(bf16[32,2,8,256]{3,2,1,0:T(8,128)(2,1)} %get-tuple-element.23) | copy-start | bytes 786436
  89.8 8.4 %collective-permute-start.10 = (bf16[32,2,8,256]{3,2,1,0:T(8,128)(2,1)}, bf16[32,2,8,256]{3,2,1,0:T(8,128)(2,1)S(1)}, u32[]{:S(2)}, u32[]{:S(2)}) collective-permute-start(bf16[32,2,8,256]{3,2,1,0:T(8,128)(2,1)} %get-tuple-element.20.refs_0_), channel_id=1, source_target_pairs={{64,0},{65,1},{66,2},{67,3},{68,4},{69,5},{70,6},{71,7},{72,8},{73... | collective-permute-start | bytes 786440 | tf_op jit(solution)/shard_map/ppermute | solution.py:28
  91.2 11.5 %collective-permute-start.21 = (f32[224,128]{1,0:T(8,128)S(1)}, f32[224,128]{1,0:T(8,128)S(1)}, u32[]{:S(2)}, u32[]{:S(2)}) collective-permute-start(f32[224,128]{1,0:T(8,128)S(1)} %add_add_fusion.2), channel_id=1, source_target_pairs={{0,12},{1,13},{2,14},{3,15},{4,0},{5,1},{6,2},{7,3},{8,4},{9,5},{1... | collective-permute-start | bytes 344072 | tf_op jit(solution)/shard_map/ppermute | solution.py:28
  95.3 9.6 %collective-permute-start.20 = (f32[224,128]{1,0:T(8,128)S(1)}, f32[224,128]{1,0:T(8,128)S(1)}, u32[]{:S(2)}, u32[]{:S(2)}) collective-permute-start(f32[224,128]{1,0:T(8,128)S(1)} %add_add_fusion.2), channel_id=1, source_target_pairs={{0,4},{1,5},{2,6},{3,7},{4,8},{5,9},{6,10},{7,11},{8,12},{9,13},{1... | collective-permute-start | bytes 344072 | tf_op jit(solution)/shard_map/ppermute | solution.py:28
  95.3 13.7 %collective-permute-start.19 = (f32[224,128]{1,0:T(8,128)S(1)}, f32[224,128]{1,0:T(8,128)S(1)}, u32[]{:S(2)}, u32[]{:S(2)}) collective-permute-start(f32[224,128]{1,0:T(8,128)S(1)} %add_add_fusion.2), channel_id=1, source_target_pairs={{0,8},{1,9},{2,10},{3,11},{4,12},{5,13},{6,14},{7,15},{8,0},{9,1},... | collective-permute-start | bytes 344072 | tf_op jit(solution)/shard_map/ppermute | solution.py:28
  96.9 12.8 %collective-permute-start.11 = (bf16[32,2,8,256]{3,2,1,0:T(8,128)(2,1)}, bf16[32,2,8,256]{3,2,1,0:T(8,128)(2,1)S(1)}, u32[]{:S(2)}, u32[]{:S(2)}) collective-permute-start(bf16[32,2,8,256]{3,2,1,0:T(8,128)(2,1)} %get-tuple-element.21), channel_id=1, source_target_pairs={{64,2},{65,3},{66,0},{67,1},{68,6},{69,7},{70,4},{71,5},{72,10},{7... | collective-permute-start | bytes 786440 | tf_op jit(solution)/shard_map/ppermute | solution.py:28
  98.2 16.7 %copy-start.10 = (bf16[32,2,8,256]{3,2,1,0:T(8,128)(2,1)}, bf16[32,2,8,256]{3,2,1,0:T(8,128)(2,1)S(1)}, u32[]{:S(2)}) copy-start(bf16[32,2,8,256]{3,2,1,0:T(8,128)(2,1)S(1)} %collective-permute-done.10.refs_2_) | copy-start | bytes 786436
  98.2 11.6 %collective-permute-start.9 = (bf16[32,2,8,256]{3,2,1,0:T(8,128)(2,1)}, bf16[32,2,8,256]{3,2,1,0:T(8,128)(2,1)S(1)}, u32[]{:S(2)}, u32[]{:S(2)}) collective-permute-start(bf16[32,2,8,256]{3,2,1,0:T(8,128)(2,1)} %get-tuple-element.21), channel_id=1, source_target_pairs={{0,2},{1,3},{2,0},{3,1},{4,6},{5,7},{6,4},{7,5},{8,10},{9,11},{10,... | collective-permute-start | bytes 786440 | tf_op jit(solution)/shard_map/ppermute | solution.py:28
  102.7 9.2 %collective-permute-start.13 = (bf16[32,2,8,256]{3,2,1,0:T(8,128)(2,1)S(1)}, bf16[32,2,8,256]{3,2,1,0:T(8,128)(2,1)S(1)}, u32[]{:S(2)}, u32[]{:S(2)}) collective-permute-start(bf16[32,2,8,256]{3,2,1,0:T(8,128)(2,1)S(1)} %copy-done.9), channel_id=1, source_target_pairs={{0,64},{1,65},{2,66},{3,67},{4,68},{5,69},{6,70},{7,71},{8,72},{9,... | collective-permute-start | bytes 786440 | tf_op jit(solution)/shard_map/ppermute | solution.py:28
  104.9 10.0 %collective-permute-start.14 = (bf16[32,2,8,256]{3,2,1,0:T(8,128)(2,1)S(1)}, bf16[32,2,8,256]{3,2,1,0:T(8,128)(2,1)S(1)}, u32[]{:S(2)}, u32[]{:S(2)}) collective-permute-start(bf16[32,2,8,256]{3,2,1,0:T(8,128)(2,1)S(1)} %copy-done.16), channel_id=1, source_target_pairs={{0,66},{1,67},{2,64},{3,65},{4,70},{5,71},{6,68},{7,69},{8,74},{9,... | collective-permute-start | bytes 786440 | tf_op jit(solution)/shard_map/ppermute | solution.py:28
  109.0 5.9 %collective-permute-start.12 = (bf16[32,2,8,256]{3,2,1,0:T(8,128)(2,1)S(1)}, bf16[32,2,8,256]{3,2,1,0:T(8,128)(2,1)S(1)}, u32[]{:S(2)}, u32[]{:S(2)}) collective-permute-start(bf16[32,2,8,256]{3,2,1,0:T(8,128)(2,1)S(1)} %copy-done.16), channel_id=1, source_target_pairs={{64,66},{65,67},{66,64},{67,65},{68,70},{69,71},{70,68},{71,69},{7... | collective-permute-start | bytes 786440 | tf_op jit(solution)/shard_map/ppermute | solution.py:28
  109.7 5.2 %copy-start.11 = (bf16[32,2,8,256]{3,2,1,0:T(8,128)(2,1)}, bf16[32,2,8,256]{3,2,1,0:T(8,128)(2,1)S(1)}, u32[]{:S(2)}) copy-start(bf16[32,2,8,256]{3,2,1,0:T(8,128)(2,1)S(1)} %collective-permute-done.11.refs_3_) | copy-start | bytes 786436
  109.7 40.2 %collective-permute-start.24 = (f32[224,128]{1,0:T(8,128)S(1)}, f32[224,128]{1,0:T(8,128)S(1)}, u32[]{:S(2)}, u32[]{:S(2)}) collective-permute-start(f32[224,128]{1,0:T(8,128)S(1)} %add_add_fusion.1), channel_id=1, source_target_pairs={{0,48},{1,49},{2,50},{3,51},{4,52},{5,53},{6,54},{7,55},{8,56},{9,... | collective-permute-start | bytes 344072 | tf_op jit(solution)/shard_map/ppermute | solution.py:28
  109.8 5.1 %copy-start.12 = (bf16[32,2,8,256]{3,2,1,0:T(8,128)(2,1)}, bf16[32,2,8,256]{3,2,1,0:T(8,128)(2,1)S(1)}, u32[]{:S(2)}) copy-start(bf16[32,2,8,256]{3,2,1,0:T(8,128)(2,1)S(1)} %collective-permute-done.9.refs_1_) | copy-start | bytes 786436
  109.8 40.1 %collective-permute-start.23 = (f32[224,128]{1,0:T(8,128)S(1)}, f32[224,128]{1,0:T(8,128)S(1)}, u32[]{:S(2)}, u32[]{:S(2)}) collective-permute-start(f32[224,128]{1,0:T(8,128)S(1)} %add_add_fusion.1), channel_id=1, source_target_pairs={{0,16},{1,17},{2,18},{3,19},{4,20},{5,21},{6,22},{7,23},{8,24},{9,... | collective-permute-start | bytes 344072 | tf_op jit(solution)/shard_map/ppermute | solution.py:28
  111.8 3.1 %copy-start.13 = (bf16[32,2,8,256]{3,2,1,0:T(8,128)(2,1)}, bf16[32,2,8,256]{3,2,1,0:T(8,128)(2,1)S(1)}, u32[]{:S(2)}) copy-start(bf16[32,2,8,256]{3,2,1,0:T(8,128)(2,1)S(1)} %collective-permute-done.13.refs_6_) | copy-start | bytes 786436
  111.8 38.1 %collective-permute-start.22 = (f32[224,128]{1,0:T(8,128)S(1)}, f32[224,128]{1,0:T(8,128)S(1)}, u32[]{:S(2)}, u32[]{:S(2)}) collective-permute-start(f32[224,128]{1,0:T(8,128)S(1)} %add_add_fusion.1), channel_id=1, source_target_pairs={{0,32},{1,33},{2,34},{3,35},{4,36},{5,37},{6,38},{7,39},{8,40},{9,... | collective-permute-start | bytes 344072 | tf_op jit(solution)/shard_map/ppermute | solution.py:28
  114.9 0.7 copy-start.14
  115.6 0.7 copy-start.15

commit v2 on v1

v2 whole, which is shorter than its diff:
```python
import functools

import jax
import jax.numpy as jnp
from jax import lax
from jax.experimental import pallas as pl
from jax.experimental.pallas import tpu as pltpu
from jax.sharding import PartitionSpec as P

AXES = ("section", "lat", "dp")
BF = jnp.bfloat16
F32 = jnp.float32
VMEM_BYTES = 20 * 1024 * 1024


def permute(value, move):
    sizes = [lax.axis_size(a) for a in AXES]
    pairs = []
    for s in range(sizes[0]):
        for l in range(sizes[1]):
            for d in range(sizes[2]):
                target = move(s, l, d)
                if target is None or not 0 <= target[1] < sizes[1]:
                    continue
                source_id = (s * sizes[1] + l) * sizes[2] + d
                target_id = (target[0] * sizes[1] + target[1]) * sizes[2] + target[2]
                pairs.append((source_id, target_id))
    return lax.ppermute(value, AXES, pairs)


def lat_move(even, odd):
    return lambda s, l, d: (s, l + (odd if l % 2 else even), d)


PARTNER = lat_move(1, -1)
NEAR_CROSS = lat_move(-1, 1)
NEAR_SAME = lat_move(-2, 2)
FAR_SAME = lat_move(2, -2)
FAR_CROSS = lat_move(3, -3)


def other_section(s, l, d):
    return (1 - s, l, d)


def ring(axis, step):
    def move(s, l, d):
        at = [l // 8, (l // 2) % 4, d * 2 + l % 2]
        at[axis] = (at[axis] + step) % 4
        return (s, at[0] * 8 + at[1] * 2 + at[2] % 2, at[2] // 2)

    return move


def other_both(s, l, d):
    return (1 - s, l ^ 1, d)


def load_cell(ref, plane, cell):
    part = ref[plane, :, cell]
    return part.astype(F32).reshape(256, 256)


def put_stack(ref, at, value):
    lane = lax.broadcasted_iota(jnp.int32, (256, 256), 1)
    before = jnp.where(lane == 0, 0.0, pltpu.roll(value, 1, 1))
    after = jnp.where(lane == 255, 0.0, pltpu.roll(value, 255, 1))
    ref[at, 0:256] = before.astype(BF)
    ref[at, 256:512] = value.astype(BF)
    ref[at, 512:768] = after.astype(BF)


def conv_cell(mat, slices):
    total = None
    for p in range(3):
        term = jnp.dot(mat[p], slices[p], preferred_element_type=F32)
        total = term if total is None else total + term
    return total


def round_bf(value):
    return value.astype(BF).astype(F32)


def slope(value):
    sig = jax.nn.sigmoid(value)
    return sig * (1.0 + value * (1.0 - sig))


def band_kernel(w_ref, wt_ref, *out_refs):
    row = lax.broadcasted_iota(jnp.int32, (256, 256), 0) % 8
    lane = lax.broadcasted_iota(jnp.int32, (256, 256), 1) % 8
    gap = lane - row
    spread = jnp.where(
        lax.broadcasted_iota(jnp.int32, (32, 256), 1) // 8
        == lax.broadcasted_iota(jnp.int32, (32, 256), 0),
        1.0,
        0.0,
    ).astype(BF)
    tall = jnp.where(
        lax.broadcasted_iota(jnp.int32, (256, 32), 0) // 8
        == lax.broadcasted_iota(jnp.int32, (256, 32), 1),
        1.0,
        0.0,
    ).astype(BF)
    for block in range(2):
        for back in range(2):
            src = wt_ref if back else w_ref
            wide = jnp.dot(
                src[block].reshape(864, 32), spread, preferred_element_type=F32
            ).astype(BF)
            for p in range(3):
                for r in range(3):
                    mat = jnp.zeros((256, 256), F32)
                    for q in range(3):
                        n = (p * 3 + q) * 3 + r
                        if back:
                            n = 26 - n
                        full = jnp.dot(
                            tall, wide[32 * n : 32 * n + 32], preferred_element_type=F32
                        )
                        mat = jnp.where(gap == q - 1, full, mat)
                    out_refs[2 * block + back][p, :, 256 * r : 256 * r + 256] = mat.astype(BF)


def make_bands(w, wt):
    return pl.pallas_call(
        band_kernel,
        out_shape=[jax.ShapeDtypeStruct((3, 256, 768), BF)] * 4,
        compiler_params=pltpu.CompilerParams(vmem_limit_bytes=VMEM_BYTES),
        name="bands",
    )(w, wt)


def valid_cell(at, pair, pairs):
    if at < 0:
        return pair > 0
    if at >= 4:
        return pair < pairs - 1
    return None


def masked(value, at, pair, pairs):
    ok = valid_cell(at, pair, pairs)
    return value if ok is None else jnp.where(ok, value, 0.0)


def pick_slab(refs, z):
    own, partner, nc, ns, fc, fs = refs
    return [(fs, fc), (nc, ns), (own, partner), (partner, own), (ns, nc), (fc, fs)]


def forward_kernel(pairs, pos_ref, own, partner, nc, ns, fc, fs, mat0, mat1,
                   xv_ref, xm_ref, pre0_ref, pre1_ref, top_own, top_oth, xv_s, xm_s):
    z = pos_ref[0]
    pair = pos_ref[1]
    even = z == 0
    slabs = pick_slab((own, partner, nc, ns, fc, fs), z)

    def xv(a):
        return (xv_ref, a + 1) if -1 <= a < 5 else (xv_s, a + 4 if a < -1 else a - 2)

    def xm(a):
        return (xm_ref, a + 1) if -1 <= a < 5 else (xm_s, a + 3 if a < -1 else a - 3)

    for a in range(-4, 8):
        j = a + 4
        first, second = slabs[j // 2]
        value = jnp.where(even, load_cell(first, 0, j % 2), load_cell(second, 0, j % 2))
        ref, at = xv(a)
        put_stack(ref, at, value)
    for a in range(-3, 7):
        near = [xv(a + p - 1) for p in range(3)]
        pre = conv_cell(mat0, [ref[at] for ref, at in near])
        if -1 <= a < 5:
            pre0_ref[a + 1] = pre
        field = near[1][0][near[1][1], 256:512].astype(F32)
        mid = round_bf(field + pre * jax.nn.sigmoid(pre))
        ref, at = xm(a)
        put_stack(ref, at, masked(mid, a, pair, pairs))
    for a in range(-2, 6):
        near = [xm(a + p - 1) for p in range(3)]
        pre = conv_cell(mat1, [ref[at] for ref, at in near])
        pre1_ref[a + 2] = pre
        if 0 <= a < 4:
            mid = near[1][0][near[1][1], 256:512].astype(F32)
            top = (mid + pre * jax.nn.sigmoid(pre)).reshape(32, 8, 256).astype(BF)
            mine = even if a < 2 else jnp.logical_not(even)

            @pl.when(mine)
            def _():
                top_own[:, a % 2] = top

            @pl.when(jnp.logical_not(mine))
            def _():
                top_oth[:, a % 2] = top


VM = pl.BlockSpec(memory_space=pltpu.MemorySpace.VMEM)
SM = pl.BlockSpec(memory_space=pltpu.MemorySpace.SMEM)
SLAB = jax.ShapeDtypeStruct((32, 2, 8, 256), BF)
STACK = jax.ShapeDtypeStruct((6, 768, 256), BF)


def run_forward(pairs, pos, slabs, mat0, mat1):
    return pl.pallas_call(
        functools.partial(forward_kernel, pairs),
        in_specs=[SM] + [VM] * 8,
        out_specs=[VM] * 6,
        out_shape=[
            STACK,
            STACK,
            jax.ShapeDtypeStruct((6, 256, 256), F32),
            jax.ShapeDtypeStruct((8, 256, 256), F32),
            SLAB,
            SLAB,
        ],
        scratch_shapes=[pltpu.VMEM((6, 768, 256), BF), pltpu.VMEM((4, 768, 256), BF)],
        compiler_params=pltpu.CompilerParams(vmem_limit_bytes=VMEM_BYTES),
        name="forward",
    )(pos, *slabs, mat0, mat1)


def kernel_grad(delta_ref, x_ref, scr, keep_ref, send_ref, kept):
    delta = jnp.concatenate([delta_ref(a) for a in range(4)], axis=1)
    for p in range(3):
        field = jnp.concatenate([x_ref[a + p] for a in range(4)], axis=1)
        full = lax.dot_general(
            delta, field, (((1,), (1,)), ((), ())), preferred_element_type=F32
        )
        for t in range(6):
            scr[6 * p + t] = full[:, 128 * t : 128 * t + 128]
    lane_row = lax.broadcasted_iota(jnp.int32, (256, 128), 0)
    fold_lane = lax.broadcasted_iota(jnp.int32, (256, 128), 1)
    total = None
    for d in range(8):
        rows = jnp.concatenate(
            [
                jnp.concatenate(
                    [scr[2 * n + t, pl.ds(d, 32, stride=8), :] for t in range(2)], axis=1
                )
                for n in range(9)
            ],
            axis=0,
        )
        high = rows.astype(BF)
        low = (rows - high.astype(F32)).astype(BF)
        fold = jnp.where(
            ((lane_row // 8) == (fold_lane % 32))
            & ((lane_row % 8) == d - 1 + fold_lane // 32)
            & (fold_lane < 96),
            1.0,
            0.0,
        ).astype(BF)
        term = jnp.dot(high, fold, preferred_element_type=F32) + jnp.dot(
            low, fold, preferred_element_type=F32
        )
        total = term if total is None else total + term

    @pl.when(kept)
    def _():
        keep_ref[...] = total

    @pl.when(jnp.logical_not(kept))
    def _():
        send_ref[...] = total


def backward_kernel(pairs, pos_ref, own, partner, nc, ns, mat, xv_ref, xm_ref, pre0_ref,
                    pre1_ref, xd0_ref, bm_ref, keep_ref, send_ref, xd1_s, scr, cot_s):
    z = pos_ref[0]
    pair = pos_ref[1]
    even = z == 0
    zero_section = pos_ref[2] == 0
    slabs = [(nc, ns), (own, partner), (partner, own), (ns, nc)]
    for a in range(-2, 6):
        j = a + 2
        first, second = slabs[j // 2]
        cot = jnp.where(even, load_cell(first, 1, j % 2), load_cell(second, 1, j % 2))
        put_stack(xd1_s, j, round_bf(cot * slope(pre1_ref[j])))
        if -1 <= a < 5:
            cot_s[a + 1] = cot
    for a in range(-1, 5):
        pre = conv_cell(mat, [xd1_s[a + 2 + p - 1] for p in range(3)])
        back = round_bf(cot_s[a + 1] + pre)
        if 0 <= a < 4:
            bm_ref[a] = back.astype(BF)
        delta = round_bf(back * slope(pre0_ref[a + 1]))
        put_stack(xd0_ref, a + 1, masked(delta, a, pair, pairs))

    kernel_grad(
        lambda a: xd0_ref[a + 1, 256:512], xv_ref, scr, keep_ref, send_ref, zero_section
    )
    kernel_grad(
        lambda a: xd1_s[a + 2, 256:512], xm_ref, scr, keep_ref, send_ref,
        jnp.logical_not(zero_section),
    )


def run_backward(pairs, pos, slabs, mats, xv, xm, pre0, pre1):
    grad = jax.ShapeDtypeStruct((288, 128), F32)
    return pl.pallas_call(
        functools.partial(backward_kernel, pairs),
        in_specs=[SM] + [VM] * 9,
        out_specs=[VM] * 4,
        out_shape=[STACK, jax.ShapeDtypeStruct((4, 256, 256), BF), grad, grad],
        scratch_shapes=[
            pltpu.VMEM((8, 768, 256), BF),
            pltpu.VMEM((18, 256, 128), F32),
            pltpu.VMEM((6, 256, 256), F32),
        ],
        compiler_params=pltpu.CompilerParams(vmem_limit_bytes=VMEM_BYTES),
        name="backward",
    )(pos, *slabs, mats, xv, xm, pre0, pre1)


def last_kernel(pos_ref, xd0_ref, bm_ref, mat, out_own, out_oth):
    even = pos_ref[0] == 0
    for a in range(4):
        pre = conv_cell(mat, [xd0_ref[a + p] for p in range(3)])
        out = (bm_ref[a].astype(F32) + pre).reshape(32, 8, 256).astype(BF)
        mine = even if a < 2 else jnp.logical_not(even)

        @pl.when(mine)
        def _():
            out_own[:, a % 2] = out

        @pl.when(jnp.logical_not(mine))
        def _():
            out_oth[:, a % 2] = out


def run_last(pos, xd0, bm, mats):
    return pl.pallas_call(
        last_kernel,
        in_specs=[SM] + [VM] * 3,
        out_specs=[VM] * 2,
        out_shape=[SLAB, SLAB],
        compiler_params=pltpu.CompilerParams(vmem_limit_bytes=VMEM_BYTES),
        name="last",
    )(pos, xd0, bm, mats)


def gather_kernel(pos_ref, own0, own1, part, sec, both, out_ref, sems):
    z = pos_ref[0]
    s = pos_ref[2]

    def piece(n, ref):
        clip = 2 * (s ^ (n // 2)) + (z ^ (n % 2))
        return pltpu.make_async_copy(ref, out_ref.at[clip], sems.at[n])

    @pl.when(s == 0)
    def _():
        piece(0, own0).start()

    @pl.when(s == 1)
    def _():
        piece(0, own1).start()

    for n, ref in ((1, part), (2, sec), (3, both)):
        piece(n, ref).start()
    for n, ref in ((0, own0), (1, part), (2, sec), (3, both)):
        piece(n, ref).wait()


def run_gather(pos, pieces):
    return pl.pallas_call(
        gather_kernel,
        in_specs=[SM] + [VM] * 5,
        out_specs=pl.BlockSpec(memory_space=pl.ANY),
        out_shape=jax.ShapeDtypeStruct((4, 32, 2, 8, 256), BF),
        scratch_shapes=[pltpu.SemaphoreType.DMA((4,))],
        compiler_params=pltpu.CompilerParams(vmem_limit_bytes=VMEM_BYTES),
        name="gather",
    )(pos, *pieces)


def unfold_kernel(a_ref, b_ref, c_ref, d_ref, out_ref):
    for n in range(9):
        rows = slice(32 * n, 32 * n + 32)
        value = (a_ref[rows] + b_ref[rows]) + (c_ref[rows] + d_ref[rows])
        p, r = divmod(n, 3)
        for q in range(3):
            out_ref[(p * 3 + q) * 3 + r] = value[:, 32 * q : 32 * q + 32]


def run_unfold(parts):
    return pl.pallas_call(
        unfold_kernel,
        out_shape=jax.ShapeDtypeStruct((27, 32, 32), F32),
        compiler_params=pltpu.CompilerParams(vmem_limit_bytes=VMEM_BYTES),
        name="unfold",
    )(*parts)


def body(volume, cotangent, weights):
    s = lax.axis_index("section")
    l = lax.axis_index("lat")
    pairs = lax.axis_size("lat") // 2
    z = l % 2
    pos = jnp.stack([z, l // 2, s]).astype(jnp.int32)

    def clip(array, at):
        return lax.dynamic_index_in_dim(array, at, 0, keepdims=False)

    same = 2 * s + z
    cross = 2 * s + (1 - z)
    mine = jnp.transpose(weights[0], (2, 3, 4, 0, 1)).reshape(27, 32, 32)
    others = permute(mine, other_section)
    same_vc = jnp.stack([clip(volume, same), clip(cotangent, same)])
    cross_vc = jnp.stack([clip(volume, cross), clip(cotangent, cross)])
    slabs = [
        same_vc,
        permute(cross_vc, PARTNER),
        permute(cross_vc, NEAR_CROSS),
        permute(same_vc, NEAR_SAME),
        permute(cross_vc[0:1], FAR_CROSS),
        permute(same_vc[0:1], FAR_SAME),
    ]
    both = jnp.where(
        s == 0, jnp.stack([mine, others]), jnp.stack([others, mine])
    )
    fwd0, bwd0, fwd1, bwd1 = make_bands(both, jnp.swapaxes(both, 2, 3))
    xv, xm, pre0, pre1, top_own, top_oth = run_forward(pairs, pos, slabs, fwd0, fwd1)
    xd0, bm, keep, send = run_backward(pairs, pos, slabs[:4], bwd1, xv, xm, pre0, pre1)
    out_own, out_oth = run_last(pos, xd0, bm, bwd0)
    total = keep + permute(send, other_section)
    for axis in (2, 1, 0):
        parts = [total] + [permute(total, ring(axis, step)) for step in (2, 1, 3)]
        if axis:
            total = (parts[0] + parts[1]) + (parts[2] + parts[3])
    at_zero = s == 0
    pieces = [
        out_own,
        top_own,
        permute(jnp.where(at_zero, out_oth, top_oth), PARTNER),
        permute(jnp.where(at_zero, top_own, out_own), other_section),
        permute(jnp.where(at_zero, top_oth, out_oth), other_both),
    ]
    field = run_gather(pos, pieces)
    grads = run_unfold(parts).reshape(3, 3, 3, 32, 32)
    return (field[None], jnp.transpose(grads, (3, 4, 0, 1, 2))[None])


def solution(mesh):
    return jax.shard_map(
        body,
        mesh=mesh,
        in_specs=(
            P("dp", None, "lat", None, None),
            P("dp", None, "lat", None, None),
            P("section", None, None, None, None, None),
        ),
        out_specs=(
            P("section", "dp", None, "lat", None, None),
            P("section", None, None, None, None, None),
        ),
        check_vma=False,
    )
```

time: 154 us -> 103 us (0.67)
  Pallas kernels: 84 us -> 28.4 us
  waiting for transfers between devices: 2.73 us -> 25.4 us
  starting transfers between devices: 53.4 us -> 39.7 us
  local copies, waits for them, and re-layouts: 7.77 us -> 4.28 us
    pallas_call x2, Pallas kernels: 42 us -> 6.72 us  [the longest x1 5.18 us: make_bands(): pl.pallas_call(band_kernel, out_shape=[jax.ShapeDtypeStruct((3, 256, 768)...]
    ppermute x25 -> x19, waiting for transfers between devices: 2.73 us -> 25.4 us  [permute(): return lax.ppermute(value, AXES, pairs)]
    ppermute x25 -> x19, starting transfers between devices: 53.4 us -> 39.7 us  [permute(): return lax.ppermute(value, AXES, pairs)]
    pallas_call x1, Pallas kernels: 19.7 us -> 8.68 us  [run_backward(): pl.pallas_call(functools.partial(backward_kernel, pairs), in_specs=[SM] +...]
    pallas_call x1, Pallas kernels: 13.4 us -> 8.5 us  [run_forward(): pl.pallas_call(functools.partial(forward_kernel, pairs), in_specs=[SM] +...]
    unnamed x34 -> x4, local copies, waits for them, and re-layouts: 3.58 us -> 0.01 us
    pallas_call x1, Pallas kernels: 7.13 us -> 3.59 us  [run_last(): pl.pallas_call(last_kernel, in_specs=[SM] + [VM] * 3, out_specs=[VM] * 2,...]
    dynamic_slice x0 -> x2, local copies, waits for them, and re-layouts: none -> 2.87 us  [clip(): return lax.dynamic_index_in_dim(array, at, 0, keepdims=False)]
  transfers between devices with their start and end apart: 25 -> 19, of which waited for: 3 -> 8; matrix products, arithmetic and copies ran while one was open for 3% -> 5% of each run, Pallas kernels for 41% -> 10%
where the time goes in v2:
time: 103 us
  starting transfers between devices  39.7 us (39%)
  Pallas kernels  28.4 us (28%)
  waiting for transfers between devices  25.4 us (25%)
  local copies, waits for them, and re-layouts  4.28 us (4%)
  other arithmetic  4.25 us (4%)
    ppermute x19, starting transfers between devices, permute(): return lax.ppermute(value, AXES, pairs)  39.7 us
    ppermute x19, waiting for transfers between devices, permute(): return lax.ppermute(value, AXES, pairs)  25.4 us
    pallas_call x1, Pallas kernels, run_backward(): pl.pallas_call(functools.partial(backward_kernel, pairs), in_specs=[SM] +...  8.68 us
    pallas_call x1, Pallas kernels, run_forward(): pl.pallas_call(functools.partial(forward_kernel, pairs), in_specs=[SM] +...  8.5 us
    pallas_call x1, Pallas kernels, make_bands(): pl.pallas_call(band_kernel, out_shape=[jax.ShapeDtypeStruct((3, 256, 768)...  5.18 us
    pallas_call x1, Pallas kernels, run_last(): pl.pallas_call(last_kernel, in_specs=[SM] + [VM] * 3, out_specs=[VM] * 2,...  3.59 us
    dynamic_slice x2, local copies, waits for them, and re-layouts, clip(): return lax.dynamic_index_in_dim(array, at, 0, keepdims=False)  2.87 us
  transfers between devices with their start and end apart: 19, of which 8 were waited for; matrix products, arithmetic and copies ran while one was open for 5% of the time, Pallas kernels for 10%

profile of v2, /device:TPU:0, one launch (start us, length us, event | category | flops | bytes accessed | tf_op | source)
XLA Modules:
  0.0 102.9 jit_solution(1792750449436546399)
XLA Ops:
  0.7 1.8 %constant_dynamic-slice_fusion.1 = (bf16[1,32,2,8,256]{4,3,2,1,0:T(8,128)(2,1)}, bf16[1,32,2,8,256]{4,3,2,1,0:T(8,128)(2,1)S(1)}) fusion(bf16[4,32,2,8,256]{4,3,2,1,0:T(8,128)(2,1)} %param.3, s32[]{:T(128)S(6)} %select_n.47, s32[]{:T(128)S(6)} %select_n.46), kind=kLoop, calls=%fused_computation.9 | loop fusion | bytes 1048584 | tf_op jit(solution)/shard_map/jit(dynamic_index_in_dim)/dynamic_slice | solution.py:404
  2.4 0.0 copy-start.1
  2.4 1.1 %constant_dynamic-slice_fusion = (bf16[1,32,2,8,256]{4,3,2,1,0:T(8,128)(2,1)S(1)}, bf16[1,32,2,8,256]{4,3,2,1,0:T(8,128)(2,1)S(1)}) fusion(bf16[4,32,2,8,256]{4,3,2,1,0:T(8,128)(2,1)} %param.4, s32[]{:T(128)S(6)} %select_n.47, s32[]{:T(128)S(6)} %select_n.46), kind=kLoop, calls=%fused_computation.8 | loop fusion | bytes 1048584 | tf_op jit(solution)/shard_map/jit(dynamic_index_in_dim)/dynamic_slice | solution.py:404
  3.5 0.1 pad_maximum_fusion.own
  3.6 1.3 %collective-permute-start.2 = (bf16[2,32,2,8,256]{4,3,2,1,0:T(8,128)(2,1)S(1)}, bf16[2,32,2,8,256]{4,3,2,1,0:T(8,128)(2,1)S(1)}, u32[]{:S(2)}, u32[]{:S(2)}) collective-permute-start(bf16[2,32,2,8,256]{4,3,2,1,0:T(8,128)(2,1)S(1)} %pad_maximum_fusion.own), channel_id=1, source_target_pairs={{2,6},{3,7},{4,0},{5,1},{6,10},{7,11},{8,4},{9,5},{10,14},{11,15},... | collective-permute-start | bytes 1572872 | tf_op jit(solution)/shard_map/ppermute | solution.py:28
  4.9 1.8 %pad_maximum_fusion.1 = bf16[2,32,2,8,256]{4,3,2,1,0:T(8,128)(2,1)} fusion(bf16[1,32,2,8,256]{4,3,2,1,0:T(8,128)(2,1)S(1)} %get-tuple-element.36, bf16[1,32,2,8,256]{4,3,2,1,0:T(8,128)(2,1)} %get-tuple-element.34), kind=kLoop, calls=%fused_computation.1 | loop fusion | flops 262144 | bytes 1048576 | tf_op jit(solution)/shard_map/stack | solution.py:411
  6.7 0.7 collective-permute-start.1
  7.4 5.6 %collective-permute-start = (bf16[2,32,2,8,256]{4,3,2,1,0:T(8,128)(2,1)}, bf16[2,32,2,8,256]{4,3,2,1,0:T(8,128)(2,1)S(1)}, u32[]{:S(2)}, u32[]{:S(2)}) collective-permute-start(bf16[2,32,2,8,256]{4,3,2,1,0:T(8,128)(2,1)} %pad_maximum_fusion.1), channel_id=1, source_target_pairs={{0,2},{1,3},{2,0},{3,1},{4,6},{5,7},{6,4},{7,5},{8,10},{9,11},{10,... | collective-permute-start | bytes 1572872 | tf_op jit(solution)/shard_map/ppermute | solution.py:28
  12.9 0.0 copy-done.1
  12.9 0.2 copy.5
  13.1 0.1 collective-permute-start.3
  13.2 4.8 %collective-permute-start.4 = (bf16[1,32,2,8,256]{4,3,2,1,0:T(8,128)(2,1)}, bf16[1,32,2,8,256]{4,3,2,1,0:T(8,128)(2,1)S(1)}, u32[]{:S(2)}, u32[]{:S(2)}) collective-permute-start(bf16[1,32,2,8,256]{4,3,2,1,0:T(8,128)(2,1)} %get-tuple-element.34), channel_id=1, source_target_pairs={{0,6},{1,7},{4,10},{5,11},{6,0},{7,1},{8,14},{9,15},{10,4},{11,5},... | collective-permute-start | bytes 786440 | tf_op jit(solution)/shard_map/ppermute | solution.py:28
  18.0 0.0 collective-permute-done.3
  18.0 0.0 copy-start
  18.0 3.5 %collective-permute-start.5 = (bf16[1,32,2,8,256]{4,3,2,1,0:T(8,128)(2,1)S(1)}, bf16[1,32,2,8,256]{4,3,2,1,0:T(8,128)(2,1)S(1)}, u32[]{:S(2)}, u32[]{:S(2)}) collective-permute-start(bf16[1,32,2,8,256]{4,3,2,1,0:T(8,128)(2,1)S(1)} %get-tuple-element.35), channel_id=1, source_target_pairs={{0,4},{1,5},{4,8},{5,9},{6,2},{7,3},{8,12},{9,13},{10,6},{11,7},{1... | collective-permute-start | bytes 786440 | tf_op jit(solution)/shard_map/ppermute | solution.py:28
  21.5 0.1 pad_add_fusion.pos_ref
  21.6 0.0 copy-done
  21.6 0.9 maximum_select_fusion
  22.5 1.2 %copy.7.w_ref = bf16[2,27,32,32]{3,2,1,0:T(8,128)(2,1)S(1)} copy(bf16[2,27,32,32]{2,3,1,0:T(8,128)(2,1)} %maximum_select_fusion) | data formatting | bytes 221184 | tf_op jit(solution)/shard_map/jit(_where)/select_n | solution.py:420
  23.8 1.3 %fusion.wt_ref = bf16[2,27,32,32]{3,2,1,0:T(8,128)(2,1)S(1)} fusion(bf16[1,27,32,32]{2,3,1,0:T(8,128)(2,1)S(1)} %bitcast.19, bf16[1,27,32,32]{2,3,1,0:T(8,128)(2,1)} %bitcast.22, pred[]{:T(512)S(6)} %eq.6), kind=kLoop, calls=%fused_computation.13 | loop fusion | flops 165888 | bytes 221185 | tf_op jit(solution)/shard_map/transpose | solution.py:423
  25.0 5.2 %bands.1 = (bf16[3,256,768]{2,1,0:T(8,128)(2,1)S(1)}, bf16[3,256,768]{2,1,0:T(8,128)(2,1)S(1)}, bf16[3,256,768]{2,1,0:T(8,128)(2,1)S(1)}, bf16[3,256,768]{2,1,0:T(8,128)(2,1)S(1)}) custom-call(bf16[2,27,32,32]{3,2,1,0:T(8,128)(2,1)S(1)} %copy.7.w_ref, bf16[2,27,32,32]{3,2,1,0:T(8,128)(2,1)S(1)} %fusion.wt_ref), custom_call_target="tpu_custom_call" | custom-call | tf_op jit(solution)/shard_map/bands/pallas_call | solution.py:127
  30.2 0.0 collective-permute-done.4.fc
  30.2 3.9 %collective-permute-done.5.fs = bf16[1,32,2,8,256]{4,3,2,1,0:T(8,128)(2,1)S(1)} collective-permute-done((bf16[1,32,2,8,256]{4,3,2,1,0:T(8,128)(2,1)S(1)}, bf16[1,32,2,8,256]{4,3,2,1,0:T(8,128)(2,1)S(1)}, u32[]{:S(2)}, u32[]{:S(2)}) %collective-permute-start.5) | collective-permute-done | bytes 262176 | tf_op jit(solution)/shard_map/ppermute | solution.py:28
  34.1 0.0 collective-permute-done.2.ns
  34.1 0.0 collective-permute-done.1.nc
  34.1 1.3 %collective-permute-done.partner = bf16[2,32,2,8,256]{4,3,2,1,0:T(8,128)(2,1)S(1)} collective-permute-done((bf16[2,32,2,8,256]{4,3,2,1,0:T(8,128)(2,1)}, bf16[2,32,2,8,256]{4,3,2,1,0:T(8,128)(2,1)S(1)}, u32[]{:S(2)}, u32[]{:S(2)}) %collective-permute-start) | collective-permute-done | bytes 524320 | tf_op jit(solution)/shard_map/ppermute | solution.py:28
  35.4 8.5 %forward.1 = (bf16[6,768,256]{2,1,0:T(8,128)(2,1)S(1)}, bf16[6,768,256]{2,1,0:T(8,128)(2,1)S(1)}, f32[6,256,256]{2,1,0:T(8,128)S(1)}, f32[8,256,256]{2,1,0:T(8,1...) custom-call(s32[3]{0:T(128)S(1)} %pad_add_fusion.pos_ref, ...), custom_call_target="tpu_custom_call" | custom-call | tf_op jit(solution)/shard_map/forward/pallas_call | solution.py:206
  43.9 8.7 %backward.1 = (bf16[6,768,256]{2,1,0:T(8,128)(2,1)S(1)}, bf16[4,256,256]{2,1,0:T(8,128)(2,1)S(1)}, f32[288,128]{1,0:T(8,128)S(1)}, f32[288,128]{1,0:T(8,128)S(1)}) custom-call(s32[3]{0:T(128)S(1)} %pad_add_fusion.pos_ref, bf16[2,32,2,8,256]{4,3,2,1,0:T(8,128)(2,1)S(1)} %pad_maximum_fusion.own, bf16[2,32,2,8,256]{4,3,2,1,0:T(8,128)(2,1)S(1)} %collective-permute-done.partner, ...), custom_call_target="tpu_custom_call" | custom-call | tf_op jit(solution)/shard_map/backward/pallas_call | solution.py:302
  52.6 0.1 collective-permute-start.9
  52.7 3.6 %last.1 = (bf16[32,2,8,256]{3,2,1,0:T(8,128)(2,1)S(1)}, bf16[32,2,8,256]{3,2,1,0:T(8,128)(2,1)S(1)}) custom-call(s32[3]{0:T(128)S(1)} %pad_add_fusion.pos_ref, bf16[6,768,256]{2,1,0:T(8,128)(2,1)S(1)} %get-tuple-element.25.xd0_ref, bf16[4,256,256]{2,1,0:T(8,128)(2,1)S(1)} %get-tuple-element.26.bm_ref, bf16[3,256,768]{2,1,0:T(8,128)(2,1)S(1)} %get-tuple-element.27.mat), custom_call_target="tpu_custom_call" | custom-call | tf_op jit(solution)/shard_map/last/pallas_call | solution.py:334
  56.3 0.0 collective-permute-done.9
  56.3 4.6 %collective-permute-start.12 = (f32[288,128]{1,0:T(8,128)S(1)}, f32[288,128]{1,0:T(8,128)S(1)}, u32[]{:S(2)}, u32[]{:S(2)}) collective-permute-start(f32[288,128]{1,0:T(8,128)S(1)} %add.46), channel_id=1, source_target_pairs={{0,3},{1,2},{2,0},{3,1},{4,7},{5,6},{6,4},{7,5},{8,11},{9,10},{10,... | collective-permute-start | bytes 442376 | tf_op jit(solution)/shard_map/ppermute | solution.py:28
  60.9 0.0 collective-permute-start.11
  60.9 1.5 %collective-permute-start.10 = (f32[288,128]{1,0:T(8,128)S(1)}, f32[288,128]{1,0:T(8,128)S(1)}, u32[]{:S(2)}, u32[]{:S(2)}) collective-permute-start(f32[288,128]{1,0:T(8,128)S(1)} %add.46), channel_id=1, source_target_pairs={{0,1},{1,0},{2,3},{3,2},{4,5},{5,4},{6,7},{7,6},{8,9},{9,8},{10,11... | collective-permute-start | bytes 442376 | tf_op jit(solution)/shard_map/ppermute | solution.py:28
  62.5 0.1 collective-permute-start.7
  62.5 2.1 %collective-permute-done.12 = f32[288,128]{1,0:T(8,128)S(1)} collective-permute-done((f32[288,128]{1,0:T(8,128)S(1)}, f32[288,128]{1,0:T(8,128)S(1)}, u32[]{:S(2)}, u32[]{:S(2)}) %collective-permute-start.12) | collective-permute-done | bytes 147488 | tf_op jit(solution)/shard_map/ppermute | solution.py:28
  64.7 6.5 %collective-permute-done.11 = f32[288,128]{1,0:T(8,128)S(1)} collective-permute-done((f32[288,128]{1,0:T(8,128)S(1)}, f32[288,128]{1,0:T(8,128)S(1)}, u32[]{:S(2)}, u32[]{:S(2)}) %collective-permute-start.11) | collective-permute-done | bytes 147488 | tf_op jit(solution)/shard_map/ppermute | solution.py:28
  71.2 0.0 collective-permute-done.10
  71.3 10.8 %collective-permute-start.15 = (f32[288,128]{1,0:T(8,128)S(1)}, f32[288,128]{1,0:T(8,128)S(1)}, u32[]{:S(2)}, u32[]{:S(2)}) collective-permute-start(f32[288,128]{1,0:T(8,128)S(1)} %add_add_fusion.1), channel_id=1, source_target_pairs={{0,12},{1,13},{2,14},{3,15},{4,0},{5,1},{6,2},{7,3},{8,4},{9,5},{1... | collective-permute-start | bytes 442376 | tf_op jit(solution)/shard_map/ppermute | solution.py:28
  82.0 0.0 collective-permute-start.14
  82.0 1.5 %collective-permute-start.13 = (f32[288,128]{1,0:T(8,128)S(1)}, f32[288,128]{1,0:T(8,128)S(1)}, u32[]{:S(2)}, u32[]{:S(2)}) collective-permute-start(f32[288,128]{1,0:T(8,128)S(1)} %add_add_fusion.1), channel_id=1, source_target_pairs={{0,8},{1,9},{2,10},{3,11},{4,12},{5,13},{6,14},{7,15},{8,0},{9,1},... | collective-permute-start | bytes 442376 | tf_op jit(solution)/shard_map/ppermute | solution.py:28
  83.6 0.1 collective-permute-start.8
  83.7 1.0 collective-permute-done.15
  84.7 0.0 collective-permute-start.6
  84.7 6.5 %collective-permute-done.14 = f32[288,128]{1,0:T(8,128)S(1)} collective-permute-done((f32[288,128]{1,0:T(8,128)S(1)}, f32[288,128]{1,0:T(8,128)S(1)}, u32[]{:S(2)}, u32[]{:S(2)}) %collective-permute-start.14) | collective-permute-done | bytes 147488 | tf_op jit(solution)/shard_map/ppermute | solution.py:28
  91.2 0.0 collective-permute-done.13
  91.3 0.1 collective-permute-start.18
  91.4 2.0 %collective-permute-start.17 = (f32[288,128]{1,0:T(8,128)S(1)}, f32[288,128]{1,0:T(8,128)S(1)}, u32[]{:S(2)}, u32[]{:S(2)}) collective-permute-start(f32[288,128]{1,0:T(8,128)S(1)} %add_add_fusion.a_ref), channel_id=1, source_target_pairs={{0,16},{1,17},{2,18},{3,19},{4,20},{5,21},{6,22},{7,23},{8,24},{9,... | collective-permute-start | bytes 442376 | tf_op jit(solution)/shard_map/ppermute | solution.py:28
  93.4 0.0 collective-permute-done.7.sec
  93.4 3.0 %collective-permute-start.16 = (f32[288,128]{1,0:T(8,128)S(1)}, f32[288,128]{1,0:T(8,128)S(1)}, u32[]{:S(2)}, u32[]{:S(2)}) collective-permute-start(f32[288,128]{1,0:T(8,128)S(1)} %add_add_fusion.a_ref), channel_id=1, source_target_pairs={{0,32},{1,33},{2,34},{3,35},{4,36},{5,37},{6,38},{7,39},{8,40},{9,... | collective-permute-start | bytes 442376 | tf_op jit(solution)/shard_map/ppermute | solution.py:28
  96.4 0.0 collective-permute-done.8.both
  96.4 0.0 collective-permute-done.6.part
  96.4 1.5 %gather.1 = bf16[4,32,2,8,256]{4,3,2,1,0:T(8,128)(2,1)} custom-call(s32[3]{0:T(128)S(1)} %pad_add_fusion.pos_ref, bf16[32,2,8,256]{3,2,1,0:T(8,128)(2,1)S(1)} %get-tuple-element.28.own0, bf16[32,2,8,256]{3,2,1,0:T(8,128)(2,1)S(1)} %get-tuple-element.29.own1, bf16[32,2,8,256]{3,2,1,0:T(8,128)(2,1)S(1)} %collective-permute-done.6.part, ...), custom_call_target="tpu_custom_call" | custom-call | tf_op jit(solution)/shard_map/gather/pallas_call | solution.py:367
  98.0 0.0 collective-permute-done.18.d_ref
  98.0 1.5 %collective-permute-done.17.c_ref = f32[288,128]{1,0:T(8,128)S(1)} collective-permute-done((f32[288,128]{1,0:T(8,128)S(1)}, f32[288,128]{1,0:T(8,128)S(1)}, u32[]{:S(2)}, u32[]{:S(2)}) %collective-permute-start.17) | collective-permute-done | bytes 147488 | tf_op jit(solution)/shard_map/ppermute | solution.py:28
  99.5 2.6 %collective-permute-done.16.b_ref = f32[288,128]{1,0:T(8,128)S(1)} collective-permute-done((f32[288,128]{1,0:T(8,128)S(1)}, f32[288,128]{1,0:T(8,128)S(1)}, u32[]{:S(2)}, u32[]{:S(2)}) %collective-permute-start.16) | collective-permute-done | bytes 147488 | tf_op jit(solution)/shard_map/ppermute | solution.py:28
  102.0 0.9 unfold.1
  (5 shorter events, 0.2 us)
Async XLA Ops:
  2.4 10.5 %copy-start.1 = (bf16[1,32,32,3,3,3]{2,1,5,4,3,0:T(8,128)(2,1)S(1)}, bf16[1,32,32,3,3,3]{2,1,5,4,3,0:T(8,128)(2,1)}, u32[]{:S(2)}) copy-start(bf16[1,32,32,3,3,3]{2,1,5,4,3,0:T(8,128)(2,1)} %param.5) | copy-start | bytes 165892
  3.6 30.5 %collective-permute-start.2 = (bf16[2,32,2,8,256]{4,3,2,1,0:T(8,128)(2,1)S(1)}, bf16[2,32,2,8,256]{4,3,2,1,0:T(8,128)(2,1)S(1)}, u32[]{:S(2)}, u32[]{:S(2)}) collective-permute-start(bf16[2,32,2,8,256]{4,3,2,1,0:T(8,128)(2,1)S(1)} %pad_maximum_fusion.own), channel_id=1, source_target_pairs={{2,6},{3,7},{4,0},{5,1},{6,10},{7,11},{8,4},{9,5},{10,14},{11,15},... | collective-permute-start | bytes 1572872 | tf_op jit(solution)/shard_map/ppermute | solution.py:28
  6.7 27.4 %collective-permute-start.1 = (bf16[2,32,2,8,256]{4,3,2,1,0:T(8,128)(2,1)}, bf16[2,32,2,8,256]{4,3,2,1,0:T(8,128)(2,1)S(1)}, u32[]{:S(2)}, u32[]{:S(2)}) collective-permute-start(bf16[2,32,2,8,256]{4,3,2,1,0:T(8,128)(2,1)} %pad_maximum_fusion.1), channel_id=1, source_target_pairs={{2,4},{3,5},{4,2},{5,3},{6,8},{7,9},{8,6},{9,7},{10,12},{11,13},{1... | collective-permute-start | bytes 1572872 | tf_op jit(solution)/shard_map/ppermute | solution.py:28
  7.4 28.0 %collective-permute-start = (bf16[2,32,2,8,256]{4,3,2,1,0:T(8,128)(2,1)}, bf16[2,32,2,8,256]{4,3,2,1,0:T(8,128)(2,1)S(1)}, u32[]{:S(2)}, u32[]{:S(2)}) collective-permute-start(bf16[2,32,2,8,256]{4,3,2,1,0:T(8,128)(2,1)} %pad_maximum_fusion.1), channel_id=1, source_target_pairs={{0,2},{1,3},{2,0},{3,1},{4,6},{5,7},{6,4},{7,5},{8,10},{9,11},{10,... | collective-permute-start | bytes 1572872 | tf_op jit(solution)/shard_map/ppermute | solution.py:28
  13.1 4.9 %collective-permute-start.3 = (bf16[27,32,32]{1,2,0:T(8,128)(2,1)S(1)}, bf16[27,32,32]{1,2,0:T(8,128)(2,1)S(1)}, u32[]{:S(2)}, u32[]{:S(2)}) collective-permute-start(bf16[27,32,32]{1,2,0:T(8,128)(2,1)S(1)} %bitcast.17), channel_id=1, source_target_pairs={{0,64},{1,65},{2,66},{3,67},{4,68},{5,69},{6,70},{7,71},{8,72},{9,... | collective-permute-start | bytes 165896 | tf_op jit(solution)/shard_map/ppermute | solution.py:28
  13.2 17.0 %collective-permute-start.4 = (bf16[1,32,2,8,256]{4,3,2,1,0:T(8,128)(2,1)}, bf16[1,32,2,8,256]{4,3,2,1,0:T(8,128)(2,1)S(1)}, u32[]{:S(2)}, u32[]{:S(2)}) collective-permute-start(bf16[1,32,2,8,256]{4,3,2,1,0:T(8,128)(2,1)} %get-tuple-element.34), channel_id=1, source_target_pairs={{0,6},{1,7},{4,10},{5,11},{6,0},{7,1},{8,14},{9,15},{10,4},{11,5},... | collective-permute-start | bytes 786440 | tf_op jit(solution)/shard_map/ppermute | solution.py:28
  18.0 3.6 %copy-start = (bf16[27,32,32]{1,2,0:T(8,128)(2,1)}, bf16[27,32,32]{1,2,0:T(8,128)(2,1)S(1)}, u32[]{:S(2)}) copy-start(bf16[27,32,32]{1,2,0:T(8,128)(2,1)S(1)} %collective-permute-done.3) | copy-start | bytes 165892
  18.0 16.0 %collective-permute-start.5 = (bf16[1,32,2,8,256]{4,3,2,1,0:T(8,128)(2,1)S(1)}, bf16[1,32,2,8,256]{4,3,2,1,0:T(8,128)(2,1)S(1)}, u32[]{:S(2)}, u32[]{:S(2)}) collective-permute-start(bf16[1,32,2,8,256]{4,3,2,1,0:T(8,128)(2,1)S(1)} %get-tuple-element.35), channel_id=1, source_target_pairs={{0,4},{1,5},{4,8},{5,9},{6,2},{7,3},{8,12},{9,13},{10,6},{11,7},{1... | collective-permute-start | bytes 786440 | tf_op jit(solution)/shard_map/ppermute | solution.py:28
  52.6 3.7 %collective-permute-start.9 = (f32[288,128]{1,0:T(8,128)S(1)}, f32[288,128]{1,0:T(8,128)S(1)}, u32[]{:S(2)}, u32[]{:S(2)}) collective-permute-start(f32[288,128]{1,0:T(8,128)S(1)} %get-tuple-element.33), channel_id=1, source_target_pairs={{0,64},{1,65},{2,66},{3,67},{4,68},{5,69},{6,70},{7,71},{8,72},{9,... | collective-permute-start | bytes 442376 | tf_op jit(solution)/shard_map/ppermute | solution.py:28
  56.3 8.4 %collective-permute-start.12 = (f32[288,128]{1,0:T(8,128)S(1)}, f32[288,128]{1,0:T(8,128)S(1)}, u32[]{:S(2)}, u32[]{:S(2)}) collective-permute-start(f32[288,128]{1,0:T(8,128)S(1)} %add.46), channel_id=1, source_target_pairs={{0,3},{1,2},{2,0},{3,1},{4,7},{5,6},{6,4},{7,5},{8,11},{9,10},{10,... | collective-permute-start | bytes 442376 | tf_op jit(solution)/shard_map/ppermute | solution.py:28
  60.9 10.3 %collective-permute-start.11 = (f32[288,128]{1,0:T(8,128)S(1)}, f32[288,128]{1,0:T(8,128)S(1)}, u32[]{:S(2)}, u32[]{:S(2)}) collective-permute-start(f32[288,128]{1,0:T(8,128)S(1)} %add.46), channel_id=1, source_target_pairs={{0,2},{1,3},{2,1},{3,0},{4,6},{5,7},{6,5},{7,4},{8,10},{9,11},{10,... | collective-permute-start | bytes 442376 | tf_op jit(solution)/shard_map/ppermute | solution.py:28
  60.9 10.3 %collective-permute-start.10 = (f32[288,128]{1,0:T(8,128)S(1)}, f32[288,128]{1,0:T(8,128)S(1)}, u32[]{:S(2)}, u32[]{:S(2)}) collective-permute-start(f32[288,128]{1,0:T(8,128)S(1)} %add.46), channel_id=1, source_target_pairs={{0,1},{1,0},{2,3},{3,2},{4,5},{5,4},{6,7},{7,6},{8,9},{9,8},{10,11... | collective-permute-start | bytes 442376 | tf_op jit(solution)/shard_map/ppermute | solution.py:28
  62.5 30.9 %collective-permute-start.7 = (bf16[32,2,8,256]{3,2,1,0:T(8,128)(2,1)S(1)}, bf16[32,2,8,256]{3,2,1,0:T(8,128)(2,1)S(1)}, u32[]{:S(2)}, u32[]{:S(2)}) collective-permute-start(bf16[32,2,8,256]{3,2,1,0:T(8,128)(2,1)S(1)} %broadcast_select_fusion.1), channel_id=1, source_target_pairs={{0,64},{1,65},{2,66},{3,67},{4,68},{5,69},{6,70},{7,71},{8,72},{9,... | collective-permute-start | bytes 786440 | tf_op jit(solution)/shard_map/ppermute | solution.py:28
  71.3 13.5 %collective-permute-start.15 = (f32[288,128]{1,0:T(8,128)S(1)}, f32[288,128]{1,0:T(8,128)S(1)}, u32[]{:S(2)}, u32[]{:S(2)}) collective-permute-start(f32[288,128]{1,0:T(8,128)S(1)} %add_add_fusion.1), channel_id=1, source_target_pairs={{0,12},{1,13},{2,14},{3,15},{4,0},{5,1},{6,2},{7,3},{8,4},{9,5},{1... | collective-permute-start | bytes 442376 | tf_op jit(solution)/shard_map/ppermute | solution.py:28
  82.0 9.2 %collective-permute-start.14 = (f32[288,128]{1,0:T(8,128)S(1)}, f32[288,128]{1,0:T(8,128)S(1)}, u32[]{:S(2)}, u32[]{:S(2)}) collective-permute-start(f32[288,128]{1,0:T(8,128)S(1)} %add_add_fusion.1), channel_id=1, source_target_pairs={{0,4},{1,5},{2,6},{3,7},{4,8},{5,9},{6,10},{7,11},{8,12},{9,13},{1... | collective-permute-start | bytes 442376 | tf_op jit(solution)/shard_map/ppermute | solution.py:28
  82.0 9.2 %collective-permute-start.13 = (f32[288,128]{1,0:T(8,128)S(1)}, f32[288,128]{1,0:T(8,128)S(1)}, u32[]{:S(2)}, u32[]{:S(2)}) collective-permute-start(f32[288,128]{1,0:T(8,128)S(1)} %add_add_fusion.1), channel_id=1, source_target_pairs={{0,8},{1,9},{2,10},{3,11},{4,12},{5,13},{6,14},{7,15},{8,0},{9,1},... | collective-permute-start | bytes 442376 | tf_op jit(solution)/shard_map/ppermute | solution.py:28
  83.6 12.8 %collective-permute-start.8 = (bf16[32,2,8,256]{3,2,1,0:T(8,128)(2,1)S(1)}, bf16[32,2,8,256]{3,2,1,0:T(8,128)(2,1)S(1)}, u32[]{:S(2)}, u32[]{:S(2)}) collective-permute-start(bf16[32,2,8,256]{3,2,1,0:T(8,128)(2,1)S(1)} %get-tuple-element.38), channel_id=1, source_target_pairs={{0,66},{1,67},{2,64},{3,65},{4,70},{5,71},{6,68},{7,69},{8,74},{9,... | collective-permute-start | bytes 786440 | tf_op jit(solution)/shard_map/ppermute | solution.py:28
  84.7 11.7 %collective-permute-start.6 = (bf16[32,2,8,256]{3,2,1,0:T(8,128)(2,1)S(1)}, bf16[32,2,8,256]{3,2,1,0:T(8,128)(2,1)S(1)}, u32[]{:S(2)}, u32[]{:S(2)}) collective-permute-start(bf16[32,2,8,256]{3,2,1,0:T(8,128)(2,1)S(1)} %get-tuple-element.39), channel_id=1, source_target_pairs={{0,2},{1,3},{2,0},{3,1},{4,6},{5,7},{6,4},{7,5},{8,10},{9,11},{10,... | collective-permute-start | bytes 786440 | tf_op jit(solution)/shard_map/ppermute | solution.py:28
  91.3 6.7 %collective-permute-start.18 = (f32[288,128]{1,0:T(8,128)S(1)}, f32[288,128]{1,0:T(8,128)S(1)}, u32[]{:S(2)}, u32[]{:S(2)}) collective-permute-start(f32[288,128]{1,0:T(8,128)S(1)} %add_add_fusion.a_ref), channel_id=1, source_target_pairs={{0,48},{1,49},{2,50},{3,51},{4,52},{5,53},{6,54},{7,55},{8,56},{9,... | collective-permute-start | bytes 442376 | tf_op jit(solution)/shard_map/ppermute | solution.py:28
  91.4 8.1 %collective-permute-start.17 = (f32[288,128]{1,0:T(8,128)S(1)}, f32[288,128]{1,0:T(8,128)S(1)}, u32[]{:S(2)}, u32[]{:S(2)}) collective-permute-start(f32[288,128]{1,0:T(8,128)S(1)} %add_add_fusion.a_ref), channel_id=1, source_target_pairs={{0,16},{1,17},{2,18},{3,19},{4,20},{5,21},{6,22},{7,23},{8,24},{9,... | collective-permute-start | bytes 442376 | tf_op jit(solution)/shard_map/ppermute | solution.py:28
  93.4 8.7 %collective-permute-start.16 = (f32[288,128]{1,0:T(8,128)S(1)}, f32[288,128]{1,0:T(8,128)S(1)}, u32[]{:S(2)}, u32[]{:S(2)}) collective-permute-start(f32[288,128]{1,0:T(8,128)S(1)} %add_add_fusion.a_ref), channel_id=1, source_target_pairs={{0,32},{1,33},{2,34},{3,35},{4,36},{5,37},{6,38},{7,39},{8,40},{9,... | collective-permute-start | bytes 442376 | tf_op jit(solution)/shard_map/ppermute | solution.py:28
